TPU v7x, 768 devices: a whole 4x8x12 slice. The times are simulated.
768 devices in a mesh: seq: 96 (over x, z, core), head: 8 (over y).
Axes of the slice: x: 4, y: 8, z: 12, core: 2. Of those that a mesh axis runs over, the one named last changes fastest.
Arguments:
- queries: bfloat16 [98304, 4096], P(('seq', 'head')), may hold values from -5 to 5
- keys: bfloat16 [98304, 1024], P(('seq', 'head')), may hold values from -5 to 5
- values: bfloat16 [98304, 1024], P(('seq', 'head')), may hold values from -6 to 6
- upstream: bfloat16 [98304, 4096], P('seq', 'head'), may hold values from -6 to 6
- lengths: int32 [96, 8], P('seq'), may hold values from 1 to 122, as said below
- guests: int32 [96, 8], P('seq'), may hold values from 0 to 1, as said below
- advantage: float32 [96, 8], P('seq'), may hold values from -4 to 4
- partner: int32 [96], replicated, may hold values from 0 to 95, as said below
Outputs:
- grad_q: bfloat16 [98304, 4096], P(('seq', 'head'))
- grad_k: bfloat16 [98304, 1024], P(('seq', 'head'))
- grad_v: bfloat16 [98304, 1024], P(('seq', 'head'))
Inputs may be any that keep to these rules, and one draw needn't show every extreme that they name: `lengths`: every tree has a slot with a response of 122 tokens; rows of a slot beyond its length are padding. `guests`: every tree has at least one guest slot. The pairing is mutual and never pairs a tree with itself: partner[partner[i]] = i.
All inputs are finite; a program needn't handle non-finite values.
Results may differ from a plain program's by a relative error of at most 0.025.
Values may be sent and summed in bfloat16 or wider, within the bound.
No kernel may reach another device: no remote copies, remote signals or barrier semaphores. Data moves between devices by JAX's collectives and lax.ppermute only.
A program may use at most 64 MiB of HBM per device.

v0:
```python
import jax
import jax.numpy as jnp
from jax import lax
from jax.sharding import PartitionSpec as P

HEAD_DIM = 128
PROMPT = 48
RESP = 8
RESP_LEN = 122


def product(form, left, right):
    return jnp.einsum(form, left, right, preferred_element_type=jnp.float32)


def forward_block(q_blk, key_blk, val_blk, allowed):
    scaling = q_blk.shape[-1] ** (-0.5)
    scores = product("blhgd,bkhd->bhglk", q_blk, key_blk) * scaling
    scores = jnp.where(allowed, scores, -jnp.inf)
    highest = jnp.max(scores, axis=-1, keepdims=True)
    lifted = jnp.exp(scores - highest)
    prob_full = lifted / jnp.sum(lifted, axis=-1, keepdims=True)
    prob_low = prob_full.astype(jnp.bfloat16)
    output = product("bhglk,bkhd->blhgd", prob_low, val_blk)
    return (prob_full, prob_low, output)


def backward_block(prob_full, prob_low, output, q_blk, key_blk, val_blk, cot_blk):
    scaling = q_blk.shape[-1] ** (-0.5)
    grad_val = product("bhglk,blhgd->bkhd", prob_low, cot_blk)
    grad_prob = product("blhgd,bkhd->bhglk", cot_blk, val_blk)
    row_inner = jnp.sum(cot_blk.astype(jnp.float32) * output, axis=-1)
    row_inner = jnp.transpose(row_inner, (0, 2, 3, 1))[..., None]
    grad_score = prob_full * (grad_prob - row_inner) * scaling
    score_low = grad_score.astype(jnp.bfloat16)
    grad_query = product("bhglk,bkhd->blhgd", score_low, key_blk)
    grad_key = product("bhglk,blhgd->bkhd", score_low, q_blk)
    return (grad_query, grad_key, grad_val)


def tree_pass(
    q_tree, k_tree, v_tree, far_keys, far_vals, cot_tree, lens_tree, guest_tree, adv_tree
):
    heads_kv = k_tree.shape[1]
    group_size = q_tree.shape[2]
    head_width = q_tree.shape[3]
    slot_rows = jnp.arange(RESP_LEN, dtype=jnp.int32)
    valid_slot = (slot_rows[None, :] < lens_tree[:, None]).astype(jnp.float32)
    weighting = valid_slot * adv_tree[:, None]
    cot_slot = (
        cot_tree[PROMPT:]
        .astype(jnp.float32)
        .reshape(RESP, RESP_LEN, heads_kv, group_size, head_width)
    )
    cot_slot = (cot_slot * weighting[:, :, None, None, None]).astype(jnp.bfloat16)
    q_prompt = q_tree[:PROMPT][None]
    k_prompt = k_tree[:PROMPT][None]
    v_prompt = v_tree[:PROMPT][None]
    prompt_rows = jnp.arange(PROMPT, dtype=jnp.int32)
    causal = prompt_rows[:, None] >= prompt_rows[None, :]
    prob_full, prob_low, out_prompt = forward_block(q_prompt, k_prompt, v_prompt, causal)
    dq_prompt, dk_prompt, dv_prompt = backward_block(
        prob_full, prob_low, out_prompt, q_prompt, k_prompt, v_prompt, cot_tree[:PROMPT][None]
    )
    chosen = (guest_tree == 1)[:, None, None, None]
    pre_keys = jnp.where(chosen, far_keys[None], k_tree[:PROMPT][None])
    pre_vals = jnp.where(chosen, far_vals[None], v_tree[:PROMPT][None])
    keys_slot = jnp.concatenate(
        [pre_keys, k_tree[PROMPT:].reshape(RESP, RESP_LEN, heads_kv, head_width)], axis=1
    )
    vals_slot = jnp.concatenate(
        [pre_vals, v_tree[PROMPT:].reshape(RESP, RESP_LEN, heads_kv, head_width)], axis=1
    )
    columns = jnp.arange(PROMPT + RESP_LEN, dtype=jnp.int32)
    allowed = (columns[None, :] < PROMPT) | (columns[None, :] - PROMPT <= slot_rows[:, None])
    q_slot = q_tree[PROMPT:].reshape(RESP, RESP_LEN, heads_kv, group_size, head_width)
    prob_full, prob_low, out_slot = forward_block(q_slot, keys_slot, vals_slot, allowed)
    out_slot = out_slot * valid_slot[:, :, None, None, None]
    dq_slot, dk_slot, dv_slot = backward_block(
        prob_full, prob_low, out_slot, q_slot, keys_slot, vals_slot, cot_slot
    )
    guest_f = guest_tree.astype(jnp.float32)[:, None, None, None]
    own_dk = dk_prompt[0] + jnp.sum((1.0 - guest_f) * dk_slot[:, :PROMPT], axis=0)
    own_dv = dv_prompt[0] + jnp.sum((1.0 - guest_f) * dv_slot[:, :PROMPT], axis=0)
    far_dk = jnp.sum(guest_f * dk_slot[:, :PROMPT], axis=0)
    far_dv = jnp.sum(guest_f * dv_slot[:, :PROMPT], axis=0)
    grad_k = jnp.concatenate(
        [own_dk, dk_slot[:, PROMPT:].reshape(RESP * RESP_LEN, heads_kv, head_width)], axis=0
    )
    grad_v = jnp.concatenate(
        [own_dv, dv_slot[:, PROMPT:].reshape(RESP * RESP_LEN, heads_kv, head_width)], axis=0
    )
    grad_q = jnp.concatenate(
        [dq_prompt[0], dq_slot.reshape(RESP * RESP_LEN, heads_kv, group_size, head_width)], axis=0
    )
    return (grad_q, grad_k, grad_v, far_dk, far_dv)


def keep_partner(mate, pieces):
    count = pieces[0].shape[0]
    picked = (jnp.arange(count, dtype=jnp.int32) == mate).astype(jnp.float32)[:, None, None]
    first_part = jnp.sum(picked * pieces[0].astype(jnp.float32), axis=0)
    second_part = jnp.sum(picked * pieces[1].astype(jnp.float32), axis=0)
    return (first_part, second_part)


def local(queries, keys, values, upstream, lengths, guests, advantage, partner):
    q_heads, k_heads, v_heads = (
        lax.all_to_all(queries, "head", split_axis=1, concat_axis=0, tiled=True),
        lax.all_to_all(keys, "head", split_axis=1, concat_axis=0, tiled=True),
        lax.all_to_all(values, "head", split_axis=1, concat_axis=0, tiled=True),
    )
    row_total = q_heads.shape[0]
    q_width = q_heads.shape[1]
    kv_width = k_heads.shape[1]
    kv_local = kv_width // HEAD_DIM
    group_size = q_width // kv_width
    mate = partner[lax.axis_index("seq")]
    own_keys = k_heads[:PROMPT]
    own_vals = v_heads[:PROMPT]
    far_keys, far_vals = keep_partner(
        mate,
        (
            lax.all_gather(own_keys[None], "seq", axis=0, tiled=True),
            lax.all_gather(own_vals[None], "seq", axis=0, tiled=True),
        ),
    )
    far_keys = far_keys.astype(jnp.bfloat16)
    far_vals = far_vals.astype(jnp.bfloat16)
    far_keys = far_keys.reshape(PROMPT, kv_local, HEAD_DIM)
    far_vals = far_vals.reshape(PROMPT, kv_local, HEAD_DIM)
    grad_q, grad_k, grad_v, far_dk, far_dv = tree_pass(
        q_heads.reshape(row_total, kv_local, group_size, HEAD_DIM),
        k_heads.reshape(row_total, kv_local, HEAD_DIM),
        v_heads.reshape(row_total, kv_local, HEAD_DIM),
        far_keys,
        far_vals,
        upstream.reshape(row_total, kv_local, group_size, HEAD_DIM),
        lengths[0],
        guests[0],
        advantage[0],
    )
    send_keys = far_dk.reshape(PROMPT, kv_width)
    send_vals = far_dv.reshape(PROMPT, kv_width)
    back_keys, back_vals = keep_partner(
        mate,
        (
            lax.all_gather(send_keys[None], "seq", axis=0, tiled=True),
            lax.all_gather(send_vals[None], "seq", axis=0, tiled=True),
        ),
    )
    grad_k = grad_k.reshape(row_total, kv_width).at[:PROMPT].add(back_keys)
    grad_v = grad_v.reshape(row_total, kv_width).at[:PROMPT].add(back_vals)
    token_q, token_k, token_v = (
        lax.all_to_all(
            grad_q.astype(jnp.bfloat16).reshape(row_total, q_width),
            "head",
            split_axis=0,
            concat_axis=1,
            tiled=True,
        ),
        lax.all_to_all(
            grad_k.astype(jnp.bfloat16), "head", split_axis=0, concat_axis=1, tiled=True
        ),
        lax.all_to_all(
            grad_v.astype(jnp.bfloat16), "head", split_axis=0, concat_axis=1, tiled=True
        ),
    )
    return (token_q, token_k, token_v)


def solution(mesh):
    return jax.shard_map(
        local,
        mesh=mesh,
        in_specs=(
            P(("seq", "head"), None),
            P(("seq", "head"), None),
            P(("seq", "head"), None),
            P("seq", "head"),
            P("seq", None),
            P("seq", None),
            P("seq", None),
            P(),
        ),
        out_specs=(P(("seq", "head"), None), P(("seq", "head"), None), P(("seq", "head"), None)),
        check_vma=False,
    )
```

profile of v0, /device:TPU:4, one launch (start us, length us, event | category | flops | bytes accessed | tf_op | source)
XLA Modules:
  0.0 547.4 jit_solution(3285865853962189448)
XLA Ops:
  7.2 0.9 copy-done
  8.2 18.8 %all_to_all.108 = bf16[128,8,128]{2,0,1:T(8,128)(2,1)S(1)} all-to-all(bf16[128,8,128]{2,0,1:T(8,128)(2,1)S(1)} %copy_bitcast_fusion.3), channel_id=1, replica_groups=mesh['seq'=96,'head'=8] {'head'}, dimensions={1} | all-to-all | bytes 524288 | tf_op jit(solution)/shard_map/all_to_all | solution.py:110
  26.9 0.7 copy-done.5
  27.7 0.6 slice.99
  28.3 1.7 copy_bitcast_fusion.2
  30.0 3.5 all-to-all-start.2
  33.5 1.3 copy.58
  34.9 9.1 %all-to-all-done.2 = bf16[128,8,128]{2,0,1:T(8,128)(2,1)S(1)} async-done(((bf16[128,8,128]{2,0,1:T(8,128)(2,1)}), bf16[128,8,128]{2,0,1:T(8,128)(2,1)S(1)}, u32[]{:S(2)}, u32[]{:S(2)}) %all-to-all-start.2) | async-done | bytes 262176 | tf_op jit(solution)/shard_map/all_to_all | solution.py:111
  43.9 3.6 all-to-all-start.1
  47.6 0.6 slice.102
  48.8 0.6 dynamic_slice.3
  49.5 1.5 slice_convert_fusion
  50.9 1.2 compare_convert_fusion
  52.2 1.9 reshape.473
  54.1 1.9 reshape.474
  56.1 2.9 copy.70
  59.6 0.6 convert_bitcast_fusion
  60.7 0.7 fusion.56
  61.4 0.7 fusion.33
  62.3 0.8 reshape.464
  63.0 0.6 slice_bitcast_fusion.4
  63.6 10.1 %all-to-all-done.1 = bf16[128,8,512]{0,2,1:T(8,128)(2,1)S(1)} async-done(((bf16[128,8,512]{0,2,1:T(8,128)(2,1)}), bf16[128,8,512]{0,2,1:T(8,128)(2,1)S(1)}, u32[]{:S(2)}, u32[]{:S(2)}) %all-to-all-start.1) | async-done | bytes 1048608 | tf_op jit(solution)/shard_map/all_to_all | solution.py:109
  73.8 0.7 copy.59
  75.0 0.7 slice.101
  75.7 2.1 reshape.489
  77.8 2.1 copy.68
  79.9 65.5 %all-gather.9.cloned.1.call-done = bf16[4608,128]{1,0:T(8,128)(2,1)} async-done(((bf16[48,128]{1,0:T(8,128)(2,1)}), bf16[4608,128]{1,0:T(8,128)(2,1)}) %all-gather.9.cloned.1.call-update) | async-done | bytes 1179664 | tf_op jit(solution)/shard_map/all_gather | solution.py:124
  145.4 116.2 %all-gather.11.cloned.1.call-done = bf16[4608,128]{1,0:T(8,128)(2,1)} async-done(((bf16[48,128]{1,0:T(8,128)(2,1)}), bf16[4608,128]{1,0:T(8,128)(2,1)}) %all-gather.11.cloned.1.call-update) | async-done | bytes 1179664 | tf_op jit(solution)/shard_map/all_gather | solution.py:125
  261.6 2.1 fusion.6
  263.9 0.6 copy-done.10
  264.5 0.7 fusion.7
  265.2 0.8 fusion.4
  266.0 0.8 copy-done.3
  266.8 0.9 fusion.16
  267.7 0.7 copy-done.2
  268.4 1.2 fusion.8
  269.6 1.3 fusion.10
  271.5 0.9 copy-done.4
  272.4 0.7 multiply_reduce_fusion.4
  273.7 0.8 slice_bitcast_fusion.3
  274.6 1.1 fusion.66
  276.2 0.6 copy-done.18
  277.1 1.4 fusion.15
  278.5 0.7 copy.71
  279.4 1.0 pad_maximum_fusion
  280.4 6.9 %all-to-all-start.3 = ((bf16[8,128,512]{2,1,0:T(8,128)(2,1)}), bf16[8,128,512]{2,1,0:T(8,128)(2,1)S(1)}, u32[]{:S(2)}, u32[]{:S(2)}) async-start(bf16[8,128,512]{2,1,0:T(8,128)(2,1)} %bitcast.57), calls=%async_computation.3 | async-start | bytes 2097152 | tf_op jit(solution)/shard_map/all_to_all | solution.py:155
  287.3 1.1 slice.105
  288.5 1.1 bitcast_add_fusion.3
  289.6 0.7 maximum_bitcast_fusion
  290.3 95.9 %all-gather.13.cloned.1.call-done = f32[4608,128]{1,0:T(8,128)} async-done(((f32[48,128]{1,0:T(8,128)}), f32[4608,128]{1,0:T(8,128)}) %all-gather.13.cloned.1.call-update) | async-done | bytes 2359312 | tf_op jit(solution)/shard_map/all_gather | solution.py:148
  386.2 116.5 %all-gather.15.cloned.1.call-done = f32[4608,128]{1,0:T(8,128)} async-done(((f32[48,128]{1,0:T(8,128)}), f32[4608,128]{1,0:T(8,128)}) %all-gather.15.cloned.1.call-update) | async-done | bytes 2359312 | tf_op jit(solution)/shard_map/all_gather | solution.py:149
  502.7 2.8 multiply_reduce_fusion
  505.5 0.6 fusion.47
  506.1 6.7 %all-to-all-start.4 = ((bf16[8,128,128]{2,1,0:T(8,128)(2,1)}), bf16[8,128,128]{2,1,0:T(8,128)(2,1)S(1)}, u32[]{:S(2)}, u32[]{:S(2)}) async-start(bf16[8,128,128]{2,1,0:T(8,128)(2,1)} %bitcast.81), calls=%async_computation.4 | async-start | bytes 524288 | tf_op jit(solution)/shard_map/all_to_all | solution.py:162
  513.1 1.1 slice.107
  514.2 0.7 maximum_bitcast_fusion.1
  515.0 0.6 fusion.45
  515.6 9.5 %all-to-all-done.4 = bf16[8,128,128]{2,1,0:T(8,128)(2,1)S(1)} async-done(((bf16[8,128,128]{2,1,0:T(8,128)(2,1)}), bf16[8,128,128]{2,1,0:T(8,128)(2,1)S(1)}, u32[]{:S(2)}, u32[]{:S(2)}) %all-to-all-start.4) | async-done | bytes 262176 | tf_op jit(solution)/shard_map/all_to_all | solution.py:162
  525.1 3.4 all-to-all-start.5
  528.5 0.7 copy.72
  529.2 1.3 copy.77
  530.7 0.9 copy.78
  531.5 8.6 %all-to-all-done.5 = bf16[8,128,128]{2,1,0:T(8,128)(2,1)S(1)} async-done(((bf16[8,128,128]{2,1,0:T(8,128)(2,1)}), bf16[8,128,128]{2,1,0:T(8,128)(2,1)S(1)}, u32[]{:S(2)}, u32[]{:S(2)}) %all-to-all-start.5) | async-done | bytes 262176 | tf_op jit(solution)/shard_map/all_to_all | solution.py:165
  540.1 0.7 copy_bitcast_fusion.1
  (96 shorter events, 5.3 us)
Async XLA Ops:
  7.2 1.0 copy-start
  7.2 26.4 %copy-start.9 = (bf16[128,4096]{1,0:T(8,128)(2,1)S(1)}, bf16[128,4096]{1,0:T(8,128)(2,1)}, u32[]{:S(2)}) copy-start(bf16[128,4096]{1,0:T(8,128)(2,1)} %param.12) | copy-start | bytes 3145732
  7.2 138.3 %all-gather.9.cloned.1.call-start = ((), (), s32[]{:S(2)}) async-start(), calls=%async_computation.6 | async-start | bytes 1191936 | tf_op jit(solution)/shard_map/all_gather | solution.py:124
  26.9 0.7 copy-start.5
  30.0 18.8 %copy-start.32 = (s32[96]{0:T(128)S(1)}, s32[96]{0:T(128)}, u32[]{:S(2)}) copy-start(s32[96]{0:T(128)} %param.19) | copy-start | bytes 1156
  30.0 14.0 %all-to-all-start.2 = ((bf16[128,8,128]{2,0,1:T(8,128)(2,1)}), bf16[128,8,128]{2,0,1:T(8,128)(2,1)S(1)}, u32[]{:S(2)}, u32[]{:S(2)}) async-start(bf16[128,8,128]{2,0,1:T(8,128)(2,1)} %copy_bitcast_fusion.2), calls=%async_computation.2 | async-start | bytes 524288 | tf_op jit(solution)/shard_map/all_to_all | solution.py:111
  43.9 5.5 %copy-start.7 = (bf16[128,8,128]{2,0,1:T(8,128)(2,1)}, bf16[128,8,128]{2,0,1:T(8,128)(2,1)S(1)}, u32[]{:S(2)}) copy-start(bf16[128,8,128]{2,0,1:T(8,128)(2,1)S(1)} %all-to-all-done.2) | copy-start | bytes 786436
  43.9 29.8 %all-to-all-start.1 = ((bf16[128,8,512]{0,2,1:T(8,128)(2,1)}), bf16[128,8,512]{0,2,1:T(8,128)(2,1)S(1)}, u32[]{:S(2)}, u32[]{:S(2)}) async-start(bf16[128,8,512]{0,2,1:T(8,128)(2,1)} %bitcast.4), calls=%async_computation.1 | async-start | bytes 2097152 | tf_op jit(solution)/shard_map/all_to_all | solution.py:109
  47.5 214.1 %all-gather.11.cloned.1.call-start = ((), (), s32[]{:S(2)}) async-start(), calls=%async_computation.7 | async-start | bytes 1191936 | tf_op jit(solution)/shard_map/all_gather | solution.py:125
  48.3 337.9 %all-gather.13.cloned.1.call-start = ((), (), s32[]{:S(2)}) async-start(), calls=%async_computation.8 | async-start | bytes 2383872 | tf_op jit(solution)/shard_map/all_gather | solution.py:148
  56.0 3.0 copy-start.33
  56.0 4.7 copy-start.25
  56.0 5.3 copy-start.28
  56.0 5.4 copy-start.29
  56.0 6.1 %copy-start.6 = (bf16[128,8,128]{2,0,1:T(8,128)(2,1)S(1)}, bf16[128,8,128]{2,0,1:T(8,128)(2,1)}, u32[]{:S(2)}) copy-start(bf16[128,8,128]{2,0,1:T(8,128)(2,1)} %copy-done.5) | copy-start | bytes 786436
  56.1 6.2 %copy-start.8 = (bf16[128,8,128]{2,0,1:T(8,128)(2,1)S(1)}, bf16[128,8,128]{2,0,1:T(8,128)(2,1)}, u32[]{:S(2)}) copy-start(bf16[128,8,128]{2,0,1:T(8,128)(2,1)} %copy-done.7) | copy-start | bytes 786436
  75.0 4.9 copy-start.1
  77.8 186.0 %copy-start.23 = (bf16[48,128]{1,0:T(8,128)(2,1)S(1)}, bf16[48,128]{1,0:T(8,128)(2,1)}, u32[]{:S(2)}) copy-start(bf16[48,128]{1,0:T(8,128)(2,1)} %slice_bitcast_fusion.4) | copy-start | bytes 36868
  77.8 186.0 %copy-start.27 = (pred[8]{0:T(512)(128)(4,1)S(1)}, pred[8]{0:T(512)(128)(4,1)}, u32[]{:S(2)}) copy-start(pred[8]{0:T(512)(128)(4,1)} %compare_bitcast_fusion) | copy-start | bytes 28
  77.8 186.8 %copy-start.16 = (pred[122,170]{0,1:T(8,128)(4,1)S(1)}, pred[122,170]{0,1:T(8,128)(4,1)}, u32[]{:S(2)}) copy-start(pred[122,170]{0,1:T(8,128)(4,1)} %fusion.33) | copy-start | bytes 62224
  263.9 0.6 copy-start.10
  265.2 1.6 copy-start.3
  266.8 1.6 copy-start.2
  266.8 1.6 copy-start.14
  266.8 1.6 copy-start.24
  267.7 3.8 copy-start.13
  268.4 1.2 copy-start.17
  270.9 1.4 copy-start.30
  270.9 1.4 copy-start.31
  271.5 0.9 copy-start.4
  273.1 229.6 %all-gather.15.cloned.1.call-start = ((), (), s32[]{:S(2)}) async-start(), calls=%async_computation.9 | async-start | bytes 2383872 | tf_op jit(solution)/shard_map/all_gather | solution.py:149
  274.5 2.5 copy-start.21
  275.7 1.4 copy-start.11
  276.2 0.6 copy-start.18
  279.4 9.1 %copy-start.15 = (f32[48,128]{1,0:T(8,128)S(1)}, f32[48,128]{1,0:T(8,128)}, u32[]{:S(2)}) copy-start(f32[48,128]{1,0:T(8,128)} %get-tuple-element.36) | copy-start | bytes 73732
  279.4 9.1 %copy-start.19 = (bf16[4,48,48]{1,2,0:T(8,128)(2,1)S(1)}, bf16[4,48,48]{1,2,0:T(8,128)(2,1)}, u32[]{:S(2)}) copy-start(bf16[4,48,48]{1,2,0:T(8,128)(2,1)} %copy-done.18) | copy-start | bytes 55300
  280.4 222.2 %copy-start.26 = (f32[96]{0:T(128)S(1)}, f32[96]{0:T(128)}, u32[]{:S(2)}) copy-start(f32[96]{0:T(128)} %compare_convert_fusion) | copy-start | bytes 1156
  280.4 225.7 %all-to-all-start.3 = ((bf16[8,128,512]{2,1,0:T(8,128)(2,1)}), bf16[8,128,512]{2,1,0:T(8,128)(2,1)S(1)}, u32[]{:S(2)}, u32[]{:S(2)}) async-start(bf16[8,128,512]{2,1,0:T(8,128)(2,1)} %bitcast.57), calls=%async_computation.3 | async-start | bytes 2097152 | tf_op jit(solution)/shard_map/all_to_all | solution.py:155
  502.7 10.2 %copy-start.12 = (f32[1,1,4,48,48]{3,4,2,1,0:T(8,128)S(1)}, f32[1,1,4,48,48]{3,4,2,1,0:T(8,128)}, u32[]{:S(2)}) copy-start(f32[1,1,4,48,48]{3,4,2,1,0:T(8,128)} %copy-done.11) | copy-start | bytes 110596
  502.7 10.2 %copy-start.20 = (f32[48,128]{1,0:T(8,128)S(1)}, f32[48,128]{1,0:T(8,128)}, u32[]{:S(2)}) copy-start(f32[48,128]{1,0:T(8,128)} %get-tuple-element.37) | copy-start | bytes 73732
  502.7 10.2 %copy-start.22 = (bf16[6,4,8,128]{3,2,1,0:T(8,128)(2,1)S(1)}, bf16[6,4,8,128]{3,2,1,0:T(8,128)(2,1)}, u32[]{:S(2)}) copy-start(bf16[6,4,8,128]{3,2,1,0:T(8,128)(2,1)} %copy-done.21) | copy-start | bytes 147460
  506.1 19.0 %all-to-all-start.4 = ((bf16[8,128,128]{2,1,0:T(8,128)(2,1)}), bf16[8,128,128]{2,1,0:T(8,128)(2,1)S(1)}, u32[]{:S(2)}, u32[]{:S(2)}) async-start(bf16[8,128,128]{2,1,0:T(8,128)(2,1)} %bitcast.81), calls=%async_computation.4 | async-start | bytes 524288 | tf_op jit(solution)/shard_map/all_to_all | solution.py:162
  525.1 15.0 %all-to-all-start.5 = ((bf16[8,128,128]{2,1,0:T(8,128)(2,1)}), bf16[8,128,128]{2,1,0:T(8,128)(2,1)S(1)}, u32[]{:S(2)}, u32[]{:S(2)}) async-start(bf16[8,128,128]{2,1,0:T(8,128)(2,1)} %bitcast.101), calls=%async_computation.5 | async-start | bytes 524288 | tf_op jit(solution)/shard_map/all_to_all | solution.py:165
Sparse Core Ops, SparseCore 0:
  28.4 117.0 all-gather.8
  149.1 112.4 all-gather.10
  273.3 112.8 all-gather.12
  389.7 112.9 all-gather.14
where the time goes:
time: 548 us; the launch traced here: 547 us
  waiting for transfers between devices  432 us (79%)
  local copies, waits for them, and re-layouts  31.6 us (6%)
  starting transfers between devices  24.5 us (4%)
  blocking collectives  18.8 us (3%)
  other arithmetic  17.4 us (3%)
  between operations  14.3 us (3%)
  matrix products  9.01 us (2%)
    all_gather x1, waiting for transfers between devices, local(): lax.all_gather(send_vals[None], 'seq', axis=0, tiled=True)  117 us
    all_gather x1, waiting for transfers between devices, local(): lax.all_gather(own_vals[None], 'seq', axis=0, tiled=True)  116 us
    all_gather x1, waiting for transfers between devices, local(): lax.all_gather(send_keys[None], 'seq', axis=0, tiled=True)  95.9 us
    all_gather x1, waiting for transfers between devices, local(): lax.all_gather(own_keys[None], 'seq', axis=0, tiled=True)  65.5 us
    all_to_all x1, blocking collectives, local(): lax.all_to_all(keys, 'head', split_axis=1, concat_axis=0, tiled=True)  18.8 us
  transfers between devices with their start and end apart: 9, of which 8 were waited for; matrix products, arithmetic and copies ran while one was open for 8% of the time, Pallas kernels for 0%

commit v1 on v0

v1 whole, which is shorter than its diff:
```python
import jax
import jax.numpy as jnp
from jax import lax
from jax.experimental import pallas as pl
from jax.experimental.pallas import tpu as pltpu
from jax.sharding import Mesh, PartitionSpec as P

HEAD_DIM = 128
PROMPT = 48
RESP = 8
RESP_LEN = 122
ROWS = 1024
GROUP = 4
KV_HEADS = 8
WINDOW = 128
TREES = ("x", "z", "core")
PLANE = ("x", "core")
X, Z, CORE = 4, 12, 2


def attend(q_rows, keys, vals, cot, allowed):
    scaling = HEAD_DIM ** (-0.5)
    nt = (((1,), (1,)), ((), ()))
    scores = lax.dot_general(keys, q_rows, nt, preferred_element_type=jnp.float32) * scaling
    scores = jnp.where(allowed, scores, -jnp.inf)
    lifted = jnp.exp(scores - jnp.max(scores, axis=0, keepdims=True))
    probs = lifted * (1.0 / jnp.sum(lifted, axis=0, keepdims=True))
    probs_low = probs.astype(jnp.bfloat16)
    grad_probs = lax.dot_general(vals, cot, nt, preferred_element_type=jnp.float32)
    inner = jnp.sum(probs_low.astype(jnp.float32) * grad_probs, axis=0, keepdims=True)
    grad_scores = (probs * (grad_probs - inner) * scaling).astype(jnp.bfloat16)
    grad_v = jnp.dot(probs_low, cot, preferred_element_type=jnp.float32)
    grad_k = jnp.dot(grad_scores, q_rows, preferred_element_type=jnp.float32)
    tn = (((0,), (0,)), ((), ()))
    grad_q = lax.dot_general(grad_scores, keys, tn, preferred_element_type=jnp.float32)
    return grad_q, jnp.concatenate([grad_k, grad_v], axis=1)


def stack_heads(block):
    return jnp.concatenate(
        [block[:, j * HEAD_DIM : (j + 1) * HEAD_DIM] for j in range(GROUP)], axis=0
    )


def unstack_heads(block, rows):
    return jnp.concatenate([block[j * rows : (j + 1) * rows] for j in range(GROUP)], axis=1)


def attention_kernel(ints, adv, q_ref, kv_ref, cot_ref, far_in, gq_ref, gkv_ref, far_out, own_out, pre, acc):
    iota = lax.broadcasted_iota
    pre[0] = kv_ref[:PROMPT, :]
    pre[1] = far_in[ints[2 * RESP]]
    acc[1] = jnp.zeros((PROMPT, 2 * HEAD_DIM), jnp.float32)

    wide = (PROMPT, GROUP * PROMPT)
    query = iota(jnp.int32, wide, 1)
    for j in range(1, GROUP):
        query = jnp.where(query >= PROMPT, query - PROMPT, query)
    grad_q, grad_kv = attend(
        stack_heads(q_ref[:PROMPT, :]),
        pre[0, :, :HEAD_DIM],
        pre[0, :, HEAD_DIM:],
        stack_heads(cot_ref[:PROMPT, :]),
        iota(jnp.int32, wide, 0) <= query,
    )
    gq_ref[:PROMPT, :] = unstack_heads(grad_q, PROMPT).astype(jnp.bfloat16)
    gkv_ref[:PROMPT, :] = jnp.zeros((PROMPT, 2 * HEAD_DIM), jnp.bfloat16)
    acc[0] = grad_kv

    for slot in range(RESP):
        first = PROMPT + RESP_LEN * slot
        start = first // 8 * 8
        skip = first - start
        rows = slice(start, start + WINDOW)
        guest = ints[RESP + slot]
        keys = jnp.concatenate([pre[guest, :, :HEAD_DIM], kv_ref[rows, :HEAD_DIM]], axis=0)
        vals = jnp.concatenate([pre[guest, :, HEAD_DIM:], kv_ref[rows, HEAD_DIM:]], axis=0)
        token = iota(jnp.int32, (WINDOW, GROUP * HEAD_DIM), 0) - skip
        weight = jnp.where((token >= 0) & (token < ints[slot]), adv[slot], 0.0)
        cot = (cot_ref[rows, :].astype(jnp.float32) * weight).astype(jnp.bfloat16)
        shape = (PROMPT + WINDOW, GROUP * WINDOW)
        key = iota(jnp.int32, shape, 0)
        query = iota(jnp.int32, shape, 1) & (WINDOW - 1)
        allowed = (key < PROMPT) | ((key >= PROMPT + skip) & (key - PROMPT <= query))
        grad_q, grad_kv = attend(stack_heads(q_ref[rows, :]), keys, vals, stack_heads(cot), allowed)
        acc[guest] += grad_kv[:PROMPT]
        for ref, new in ((gq_ref, unstack_heads(grad_q, WINDOW)), (gkv_ref, grad_kv[PROMPT:])):
            if skip:
                old = ref[start : start + 8, :].astype(jnp.float32)
                top = jnp.where(iota(jnp.int32, old.shape, 0) < skip, old, new[:8])
                new = jnp.concatenate([top, new[8:]], axis=0)
            ref[rows, :] = new.astype(jnp.bfloat16)

    own_out[...] = acc[0]
    far = acc[1].astype(jnp.bfloat16)
    for i in range(X * CORE):
        far_out[i] = far


def attention(ints, adv, q_heads, kv_heads, cot, far):
    vmem = pl.BlockSpec(memory_space=pltpu.VMEM)
    smem = pl.BlockSpec(memory_space=pltpu.SMEM)
    width = 2 * HEAD_DIM
    return pl.pallas_call(
        attention_kernel,
        out_shape=(
            jax.ShapeDtypeStruct((ROWS, GROUP * HEAD_DIM), jnp.bfloat16),
            jax.ShapeDtypeStruct((ROWS, width), jnp.bfloat16),
            jax.ShapeDtypeStruct((X * CORE, PROMPT, width), jnp.bfloat16),
            jax.ShapeDtypeStruct((PROMPT, width), jnp.float32),
        ),
        in_specs=[smem, smem, vmem, vmem, vmem, vmem],
        out_specs=(vmem, vmem, vmem, vmem),
        scratch_shapes=[
            pltpu.VMEM((2, PROMPT, width), jnp.bfloat16),
            pltpu.VMEM((2, PROMPT, width), jnp.float32),
        ],
        cost_estimate=pl.CostEstimate(flops=10**9, transcendentals=720896, bytes_accessed=5 * 2**20),
        name="attention",
    )(ints, adv, q_heads, kv_heads, cot, far)


def pick_kernel(index, blocks, out):
    for i in range(Z):
        out[i] = blocks[index[i]]


def pick(index, blocks):
    return pl.pallas_call(
        pick_kernel,
        out_shape=jax.ShapeDtypeStruct((Z,) + blocks.shape[1:], blocks.dtype),
        in_specs=[pl.BlockSpec(memory_space=pltpu.SMEM), pl.BlockSpec(memory_space=pltpu.VMEM)],
        out_specs=pl.BlockSpec(memory_space=pltpu.VMEM),
        cost_estimate=pl.CostEstimate(flops=0, transcendentals=0, bytes_accessed=2**19),
        name="pick",
    )(index, blocks)


def exchange(copies, route):
    plane = lax.all_to_all(copies, PLANE, split_axis=0, concat_axis=0, tiled=True)
    return lax.all_to_all(pick(route, plane), "z", split_axis=0, concat_axis=0, tiled=True)


def local(queries, keys, values, upstream, lengths, guests, advantage, partner):
    rows = queries.shape[0]

    def by_head(array):
        return array.reshape(rows, KV_HEADS, -1).transpose(1, 0, 2)

    kv = jnp.concatenate([by_head(keys), by_head(values)], axis=2)
    kv = lax.all_to_all(kv, "head", split_axis=0, concat_axis=0, tiled=True).reshape(ROWS, -1)
    q = lax.all_to_all(by_head(queries), "head", split_axis=0, concat_axis=0, tiled=True)

    x, z, core = (lax.axis_index(name) for name in TREES)
    mate = partner[(x * Z + z) * CORE + core]
    column = partner[(x * Z + jnp.arange(Z)) * CORE + core]
    route = column // (Z * CORE) * CORE + column % CORE
    ints = jnp.concatenate([lengths[0], guests[0], (mate // CORE % Z)[None]]).astype(jnp.int32)

    copies = jnp.broadcast_to(kv[None, :PROMPT], (X * CORE, PROMPT, 2 * HEAD_DIM))
    far = exchange(copies, route)
    grad_q, grad_kv, far_copies, own = attention(
        ints, advantage[0], q.reshape(ROWS, -1), kv, upstream, far
    )
    back = exchange(far_copies, route)
    back = lax.dynamic_index_in_dim(back, ints[2 * RESP], 0, keepdims=False)
    prompt = (own + back.astype(jnp.float32)).astype(jnp.bfloat16)
    grad_kv = jnp.concatenate([prompt, grad_kv[PROMPT:]], axis=0)

    def by_row(array):
        array = lax.all_to_all(
            array.reshape(KV_HEADS, rows, -1), "head", split_axis=0, concat_axis=0, tiled=True
        )
        return array.transpose(1, 0, 2)

    grad_q = by_row(grad_q).reshape(rows, -1)
    grad_kv = by_row(grad_kv)
    return (
        grad_q,
        grad_kv[:, :, :HEAD_DIM].reshape(rows, -1),
        grad_kv[:, :, HEAD_DIM:].reshape(rows, -1),
    )


def solution(mesh):
    mesh = Mesh(mesh.devices.reshape(X, Z, CORE, KV_HEADS), TREES + ("head",))
    tokens = P(TREES + ("head",), None)
    trees = P(TREES, None)
    return jax.shard_map(
        local,
        mesh=mesh,
        in_specs=(tokens, tokens, tokens, P(TREES, "head"), trees, trees, trees, P()),
        out_specs=(tokens, tokens, tokens),
        check_vma=False,
    )
```

time: 548 us -> 201 us (0.37)
  the two profiles are of different devices: /device:TPU:4 before, /device:TPU:65 now
where the time goes in v1:
time: 201 us; the launch traced here: 200 us
  waiting for transfers between devices  88.1 us (44%)
  blocking collectives  54.1 us (27%)
  starting transfers between devices  31.6 us (16%)
  local copies, waits for them, and re-layouts  10.7 us (5%)
  Pallas kernels  10.1 us (5%)
  between operations  3.42 us (2%)
  other arithmetic  2.09 us (1%)
    all_to_all x2, waiting for transfers between devices, by_row(): lax.all_to_all(array.reshape(KV_HEADS, rows, -1), 'head', split_axis=0, c...  44.3 us
    all_to_all x1, waiting for transfers between devices, local(): lax.all_to_all(by_head(queries), 'head', split_axis=0, concat_axis=0, til...  26.2 us
    all_to_all x1, blocking collectives, local(): lax.all_to_all(kv, 'head', split_axis=0, concat_axis=0, tiled=True)  22.9 us
    all_to_all x1, blocking collectives, exchange(): lax.all_to_all(pick(route, plane), 'z', split_axis=0, concat_axis=0, tile...  20.9 us
    all_to_all x1, starting transfers between devices, exchange(): lax.all_to_all(pick(route, plane), 'z', split_axis=0, concat_axis=0, tile...  14.2 us
    all_to_all x1, waiting for transfers between devices, exchange(): lax.all_to_all(pick(route, plane), 'z', split_axis=0, concat_axis=0, tile...  12.9 us
    all_to_all x1, blocking collectives, exchange(): lax.all_to_all(copies, PLANE, split_axis=0, concat_axis=0, tiled=True)  10.4 us
    all_to_all x2, starting transfers between devices, by_row(): lax.all_to_all(array.reshape(KV_HEADS, rows, -1), 'head', split_axis=0, c...  7.18 us
  transfers between devices with their start and end apart: 5, of which 5 were waited for; matrix products, arithmetic and copies ran while one was open for 3% of the time, Pallas kernels for 1%

profile of v1, /device:TPU:65, one launch (start us, length us, event | category | flops | bytes accessed | tf_op | source)
XLA Modules:
  0.0 200.1 jit_solution(18159826144268286993)
XLA Ops:
  0.6 0.0 copy-start
  0.6 0.9 copy-done
  1.6 1.1 bitcast_bitcast_fusion.1
  2.7 0.1 pad_maximum_fusion
  2.7 0.0 copy-start.2
  2.8 22.9 %all_to_all.40 = bf16[8,128,256]{2,1,0:T(8,128)(2,1)S(1)} all-to-all(bf16[8,128,256]{2,1,0:T(8,128)(2,1)S(1)} %pad_maximum_fusion), channel_id=1, replica_groups=mesh['x'=4,'z'=12,'core'=2,'head'=8] {'head'}, dimensions={0} | all-to-all | bytes 1048576 | tf_op jit(solution)/shard_map/all_to_all | solution.py:151
  25.6 0.0 copy-start.5
  25.6 0.7 broadcast_in_dim.5
  26.4 6.6 %all-to-all-start.2 = ((bf16[8,48,256]{2,1,0:T(8,128)(2,1)}), bf16[8,48,256]{2,1,0:T(8,128)(2,1)S(1)}, u32[]{:S(2)}, u32[]{:S(2)}) async-start(bf16[8,48,256]{2,1,0:T(8,128)(2,1)} %broadcast_in_dim.5), calls=%async_computation.2 | async-start | bytes 393216 | tf_op jit(solution)/shard_map/all_to_all | solution.py:140
  33.0 0.0 copy-done.2
  33.0 1.1 copy.34
  34.1 0.0 copy-done.5
  34.1 4.8 %all-to-all-done.2.blocks = bf16[8,48,256]{2,1,0:T(8,128)(2,1)S(1)} async-done(((bf16[8,48,256]{2,1,0:T(8,128)(2,1)}), bf16[8,48,256]{2,1,0:T(8,128)(2,1)S(1)}, u32[]{:S(2)}, u32[]{:S(2)}) %all-to-all-start.2) | async-done | bytes 196640 | tf_op jit(solution)/shard_map/all_to_all | solution.py:140
  38.8 0.0 copy-start.4
  38.8 0.0 copy-start.1
  38.8 0.7 copy-done.4
  39.5 3.6 %all-to-all-start = ((bf16[8,128,512]{2,1,0:T(8,128)(2,1)}), bf16[8,128,512]{2,1,0:T(8,128)(2,1)S(1)}, u32[]{:S(2)}, u32[]{:S(2)}) async-start(bf16[8,128,512]{2,1,0:T(8,128)(2,1)} %bitcast.46), calls=%async_computation | async-start | bytes 2097152 | tf_op jit(solution)/shard_map/all_to_all | solution.py:152
  43.1 0.0 copy-done.1
  43.1 0.7 gather_fusion
  43.8 0.5 fusion.1.index
  44.3 1.7 pick.2
  46.0 26.2 %all-to-all-done = bf16[8,128,512]{2,1,0:T(8,128)(2,1)S(1)} async-done(((bf16[8,128,512]{2,1,0:T(8,128)(2,1)}), bf16[8,128,512]{2,1,0:T(8,128)(2,1)S(1)}, u32[]{:S(2)}, u32[]{:S(2)}) %all-to-all-start) | async-done | bytes 1048608 | tf_op jit(solution)/shard_map/all_to_all | solution.py:152
  72.2 0.0 copy-start.3
  72.2 14.2 %all-to-all-start.3 = ((bf16[12,48,256]{2,1,0:T(8,128)(2,1)}), bf16[12,48,256]{2,1,0:T(8,128)(2,1)S(1)}, u32[]{:S(2)}, u32[]{:S(2)}) async-start(bf16[12,48,256]{2,1,0:T(8,128)(2,1)} %pick.2), calls=%async_computation.3 | async-start | bytes 589824 | tf_op jit(solution)/shard_map/all_to_all | solution.py:141
  86.4 0.6 dynamic_slice.7
  89.6 0.0 copy-start.9
  89.6 0.0 copy-start.10
  89.6 0.6 copy-done.9
  90.3 0.0 copy-done.10
  90.3 0.6 pad_add_fusion.ints
  90.9 12.9 %all-to-all-done.3.far_in = bf16[12,48,256]{2,1,0:T(8,128)(2,1)S(1)} async-done(((bf16[12,48,256]{2,1,0:T(8,128)(2,1)}), bf16[12,48,256]{2,1,0:T(8,128)(2,1)S(1)}, u32[]{:S(2)}, u32[]{:S(2)}) %all-to-all-start.3) | async-done | bytes 294944 | tf_op jit(solution)/shard_map/all_to_all | solution.py:141
  103.8 0.0 copy-start.7
  103.8 0.0 copy-done.3
  103.8 0.7 copy-done.7
  104.5 6.8 %attention.1 = (bf16[1024,512]{1,0:T(8,128)(2,1)}, bf16[1024,256]{1,0:T(8,128)(2,1)}, bf16[8,48,256]{2,1,0:T(8,128)(2,1)}, f32[48,256]{1,0:T(8,128)}) custom-call(s32[17]{0:T(128)} %pad_add_fusion.ints, f32[8]{0:T(128)} %bitcast.60, bf16[1024,512]{1,0:T(8,128)(2,1)} %bitcast.52, bf16[1024,256]{1,0:T(8,128)(2,1)} %bitcast.55, bf16[1024,512]{1,0:T(8,128)(2,1)} %cot_ref.1, ...), custom_call_target="tpu_custom_call" | custom-call | flops 1000000000 | bytes 5242880 | tf_op jit(solution)/shard_map/attention/pallas_call | solution.py:104
  111.2 10.4 %all_to_all.41.blocks = bf16[8,48,256]{2,1,0:T(8,128)(2,1)} all-to-all(bf16[8,48,256]{2,1,0:T(8,128)(2,1)} %get-tuple-element.9), channel_id=1, replica_groups=mesh['x'=4,'z'=12,'core'=2,'head'=8] {'x','core'}, dimensions={0} | all-to-all | bytes 393216 | tf_op jit(solution)/shard_map/all_to_all | solution.py:140
  121.6 1.7 pick.3
  123.3 20.9 %all_to_all.42 = bf16[12,48,256]{2,1,0:T(8,128)(2,1)S(1)} all-to-all(bf16[12,48,256]{2,1,0:T(8,128)(2,1)} %pick.3), channel_id=1, replica_groups=mesh['x'=4,'z'=12,'core'=2,'head'=8] {'z'}, dimensions={0} | all-to-all | bytes 589824 | tf_op jit(solution)/shard_map/all_to_all | solution.py:141
  144.2 0.0 copy-start.6
  144.2 3.7 %all-to-all-start.4 = ((bf16[8,128,512]{2,1,0:T(8,128)(2,1)}), bf16[8,128,512]{2,1,0:T(8,128)(2,1)S(1)}, u32[]{:S(2)}, u32[]{:S(2)}) async-start(bf16[8,128,512]{2,1,0:T(8,128)(2,1)} %bitcast.11), calls=%async_computation.4 | async-start | bytes 2097152 | tf_op jit(solution)/shard_map/all_to_all | solution.py:171
  147.9 0.0 copy-done.6
  147.9 0.0 copy-start.8
  147.9 0.7 copy-done.8
  148.7 0.8 pad_maximum_fusion.1
  149.5 27.5 %all-to-all-done.4 = bf16[8,128,512]{2,1,0:T(8,128)(2,1)S(1)} async-done(((bf16[8,128,512]{2,1,0:T(8,128)(2,1)}), bf16[8,128,512]{2,1,0:T(8,128)(2,1)S(1)}, u32[]{:S(2)}, u32[]{:S(2)}) %all-to-all-start.4) | async-done | bytes 1048608 | tf_op jit(solution)/shard_map/all_to_all | solution.py:171
  177.0 3.5 %all-to-all-start.7 = ((bf16[8,128,256]{2,1,0:T(8,128)(2,1)}), bf16[8,128,256]{2,1,0:T(8,128)(2,1)S(1)}, u32[]{:S(2)}, u32[]{:S(2)}) async-start(bf16[8,128,256]{2,1,0:T(8,128)(2,1)} %bitcast.14), calls=%async_computation.7 | async-start | bytes 1048576 | tf_op jit(solution)/shard_map/all_to_all | solution.py:171
  180.5 1.1 copy.26
  181.6 16.8 %all-to-all-done.7 = bf16[8,128,256]{2,1,0:T(8,128)(2,1)S(1)} async-done(((bf16[8,128,256]{2,1,0:T(8,128)(2,1)}), bf16[8,128,256]{2,1,0:T(8,128)(2,1)S(1)}, u32[]{:S(2)}, u32[]{:S(2)}) %all-to-all-start.7) | async-done | bytes 524320 | tf_op jit(solution)/shard_map/all_to_all | solution.py:171
  198.4 0.1 slice_bitcast_fusion
  198.5 0.8 copy.35
  199.3 0.8 copy.36
  (5 shorter events, 0.1 us)
Async XLA Ops:
  0.6 1.0 copy-start
  2.7 30.2 %copy-start.2 = (bf16[128,4096]{1,0:T(8,128)(2,1)S(1)}, bf16[128,4096]{1,0:T(8,128)(2,1)}, u32[]{:S(2)}) copy-start(bf16[128,4096]{1,0:T(8,128)(2,1)} %param.8) | copy-start | bytes 3145732
  25.6 8.4 %copy-start.5 = (bf16[8,128,256]{2,1,0:T(8,128)(2,1)}, bf16[8,128,256]{2,1,0:T(8,128)(2,1)S(1)}, u32[]{:S(2)}) copy-start(bf16[8,128,256]{2,1,0:T(8,128)(2,1)S(1)} %all_to_all.40) | copy-start | bytes 1572868
  26.4 12.5 %all-to-all-start.2 = ((bf16[8,48,256]{2,1,0:T(8,128)(2,1)}), bf16[8,48,256]{2,1,0:T(8,128)(2,1)S(1)}, u32[]{:S(2)}, u32[]{:S(2)}) async-start(bf16[8,48,256]{2,1,0:T(8,128)(2,1)} %broadcast_in_dim.5), calls=%async_computation.2 | async-start | bytes 393216 | tf_op jit(solution)/shard_map/all_to_all | solution.py:140
  38.8 0.7 copy-start.4
  38.8 4.3 %copy-start.1 = (s32[96]{0:T(128)S(1)}, s32[96]{0:T(128)}, u32[]{:S(2)}) copy-start(s32[96]{0:T(128)} %param.15) | copy-start | bytes 1156
  39.5 32.7 %all-to-all-start = ((bf16[8,128,512]{2,1,0:T(8,128)(2,1)}), bf16[8,128,512]{2,1,0:T(8,128)(2,1)S(1)}, u32[]{:S(2)}, u32[]{:S(2)}) async-start(bf16[8,128,512]{2,1,0:T(8,128)(2,1)} %bitcast.46), calls=%async_computation | async-start | bytes 2097152 | tf_op jit(solution)/shard_map/all_to_all | solution.py:152
  72.2 31.6 %copy-start.3 = (bf16[8,128,512]{2,1,0:T(8,128)(2,1)}, bf16[8,128,512]{2,1,0:T(8,128)(2,1)S(1)}, u32[]{:S(2)}) copy-start(bf16[8,128,512]{2,1,0:T(8,128)(2,1)S(1)} %all-to-all-done) | copy-start | bytes 3145732
  72.2 31.6 %all-to-all-start.3 = ((bf16[12,48,256]{2,1,0:T(8,128)(2,1)}), bf16[12,48,256]{2,1,0:T(8,128)(2,1)S(1)}, u32[]{:S(2)}, u32[]{:S(2)}) async-start(bf16[12,48,256]{2,1,0:T(8,128)(2,1)} %pick.2), calls=%async_computation.3 | async-start | bytes 589824 | tf_op jit(solution)/shard_map/all_to_all | solution.py:141
  89.6 0.7 copy-start.9
  89.6 0.7 copy-start.10
  103.8 0.7 copy-start.7
  144.2 3.7 %copy-start.6 = (bf16[1024,256]{1,0:T(8,128)(2,1)S(1)}, bf16[1024,256]{1,0:T(8,128)(2,1)}, u32[]{:S(2)}) copy-start(bf16[1024,256]{1,0:T(8,128)(2,1)} %get-tuple-element.10) | copy-start | bytes 1572868
  144.2 32.8 %all-to-all-start.4 = ((bf16[8,128,512]{2,1,0:T(8,128)(2,1)}), bf16[8,128,512]{2,1,0:T(8,128)(2,1)S(1)}, u32[]{:S(2)}, u32[]{:S(2)}) async-start(bf16[8,128,512]{2,1,0:T(8,128)(2,1)} %bitcast.11), calls=%async_computation.4 | async-start | bytes 2097152 | tf_op jit(solution)/shard_map/all_to_all | solution.py:171
  147.9 0.8 copy-start.8
  177.0 21.4 %all-to-all-start.7 = ((bf16[8,128,256]{2,1,0:T(8,128)(2,1)}), bf16[8,128,256]{2,1,0:T(8,128)(2,1)S(1)}, u32[]{:S(2)}, u32[]{:S(2)}) async-start(bf16[8,128,256]{2,1,0:T(8,128)(2,1)} %bitcast.14), calls=%async_computation.7 | async-start | bytes 1048576 | tf_op jit(solution)/shard_map/all_to_all | solution.py:171

commit v2 on v1

v2 whole, which is shorter than its diff:
```python
import jax
import jax.numpy as jnp
from jax import lax
from jax.experimental import pallas as pl
from jax.experimental.pallas import tpu as pltpu
from jax.sharding import Mesh, PartitionSpec as P

HEAD_DIM = 128
PROMPT = 48
RESP = 8
RESP_LEN = 122
ROWS = 1024
GROUP = 4
KV_HEADS = 8
WINDOW = 128
Q = GROUP * HEAD_DIM
KV = 2 * HEAD_DIM
TREES = ("x", "z", "core")
PLANE = ("x", "core")
X, Z, CORE = 4, 12, 2


def attend(q_rows, keys, vals, cot, allowed):
    scaling = HEAD_DIM ** (-0.5)
    nt = (((1,), (1,)), ((), ()))
    scores = lax.dot_general(keys, q_rows, nt, preferred_element_type=jnp.float32) * scaling
    scores = jnp.where(allowed, scores, -jnp.inf)
    lifted = jnp.exp(scores - jnp.max(scores, axis=0, keepdims=True))
    probs = lifted * (1.0 / jnp.sum(lifted, axis=0, keepdims=True))
    probs_low = probs.astype(jnp.bfloat16)
    grad_probs = lax.dot_general(vals, cot, nt, preferred_element_type=jnp.float32)
    inner = jnp.sum(probs_low.astype(jnp.float32) * grad_probs, axis=0, keepdims=True)
    grad_scores = (probs * (grad_probs - inner) * scaling).astype(jnp.bfloat16)
    grad_v = jnp.dot(probs_low, cot, preferred_element_type=jnp.float32)
    grad_k = jnp.dot(grad_scores, q_rows, preferred_element_type=jnp.float32)
    tn = (((0,), (0,)), ((), ()))
    grad_q = lax.dot_general(grad_scores, keys, tn, preferred_element_type=jnp.float32)
    return grad_q, jnp.concatenate([grad_k, grad_v], axis=1)


def stack_heads(block):
    return jnp.concatenate(
        [block[:, j * HEAD_DIM : (j + 1) * HEAD_DIM] for j in range(GROUP)], axis=0
    )


def unstack_heads(block, rows):
    return jnp.concatenate([block[j * rows : (j + 1) * rows] for j in range(GROUP)], axis=1)


def attention_kernel(ints, adv, qkv, prompt, cot_ref, stay, cross, grads, far_out, own_out, pre, acc):
    iota = lax.broadcasted_iota
    pre[0] = prompt[...]
    for crossed, ref in enumerate((stay, cross)):

        @pl.when(ints[2 * RESP] == crossed)
        def _():
            pre[1] = ref[...]

    acc[1] = jnp.zeros((PROMPT, KV), jnp.float32)

    wide = (PROMPT, GROUP * PROMPT)
    query = iota(jnp.int32, wide, 1)
    for j in range(1, GROUP):
        query = jnp.where(query >= PROMPT, query - PROMPT, query)
    grad_q, grad_kv = attend(
        stack_heads(qkv[:PROMPT, :Q]),
        pre[0, :, :HEAD_DIM],
        pre[0, :, HEAD_DIM:],
        stack_heads(cot_ref[:PROMPT, :]),
        iota(jnp.int32, wide, 0) <= query,
    )
    grads[:PROMPT, :Q] = unstack_heads(grad_q, PROMPT).astype(jnp.bfloat16)
    grads[:PROMPT, Q:] = jnp.zeros((PROMPT, KV), jnp.bfloat16)
    acc[0] = grad_kv

    for slot in range(RESP):
        first = PROMPT + RESP_LEN * slot
        start = first // 8 * 8
        skip = first - start
        rows = slice(start, start + WINDOW)
        guest = ints[RESP + slot]
        keys = jnp.concatenate([pre[guest, :, :HEAD_DIM], qkv[rows, Q : Q + HEAD_DIM]], axis=0)
        vals = jnp.concatenate([pre[guest, :, HEAD_DIM:], qkv[rows, Q + HEAD_DIM :]], axis=0)
        token = iota(jnp.int32, (WINDOW, Q), 0) - skip
        weight = jnp.where((token >= 0) & (token < ints[slot]), adv[slot], 0.0)
        cot = (cot_ref[rows, :].astype(jnp.float32) * weight).astype(jnp.bfloat16)
        shape = (PROMPT + WINDOW, GROUP * WINDOW)
        key = iota(jnp.int32, shape, 0)
        query = iota(jnp.int32, shape, 1) & (WINDOW - 1)
        allowed = (key < PROMPT) | ((key >= PROMPT + skip) & (key - PROMPT <= query))
        grad_q, grad_kv = attend(stack_heads(qkv[rows, :Q]), keys, vals, stack_heads(cot), allowed)
        acc[guest] += grad_kv[:PROMPT]
        new = jnp.concatenate([unstack_heads(grad_q, WINDOW), grad_kv[PROMPT:]], axis=1)
        if skip:
            old = grads[start : start + 8, :].astype(jnp.float32)
            top = jnp.where(iota(jnp.int32, old.shape, 0) < skip, old, new[:8])
            new = jnp.concatenate([top, new[8:]], axis=0)
        grads[rows, :] = new.astype(jnp.bfloat16)

    own_out[...] = acc[0]
    far_out[...] = acc[1].astype(jnp.bfloat16)


VMEM = pl.BlockSpec(memory_space=pltpu.VMEM)
SMEM = pl.BlockSpec(memory_space=pltpu.SMEM)


def attention(ints, adv, qkv, prompt, cot, stay, cross):
    return pl.pallas_call(
        attention_kernel,
        out_shape=(
            jax.ShapeDtypeStruct((ROWS, Q + KV), jnp.bfloat16),
            jax.ShapeDtypeStruct((PROMPT, KV), jnp.bfloat16),
            jax.ShapeDtypeStruct((PROMPT, KV), jnp.float32),
        ),
        in_specs=[SMEM] * 2 + [VMEM] * 5,
        out_specs=(VMEM, VMEM, VMEM),
        scratch_shapes=[
            pltpu.VMEM((2, PROMPT, KV), jnp.bfloat16),
            pltpu.VMEM((2, PROMPT, KV), jnp.float32),
        ],
        cost_estimate=pl.CostEstimate(flops=10**9, transcendentals=720896, bytes_accessed=5 * 2**20),
        name="attention",
    )(ints, adv, qkv, prompt, cot, stay, cross)


def spread_kernel(index, blocks, *outs):
    for k, out in enumerate(outs):
        for i in range(CORE):
            out[i] = blocks[index[CORE * k + i]]


def spread(index, blocks):
    pair = jax.ShapeDtypeStruct((CORE,) + blocks.shape[1:], blocks.dtype)
    return pl.pallas_call(
        spread_kernel,
        out_shape=(pair,) * X,
        in_specs=[SMEM, VMEM],
        out_specs=(VMEM,) * X,
        cost_estimate=pl.CostEstimate(flops=0, transcendentals=0, bytes_accessed=2**19),
        name="spread",
    )(index, blocks)


def narrow_kernel(index, *refs):
    pairs, outs = refs[:X], refs[X:]
    for i, out in enumerate(outs):
        for k, pair in enumerate(pairs):

            @pl.when(index[i] == k)
            def _():
                out[...] = pair[index[CORE + i]]


def narrow(index, pairs):
    block = jax.ShapeDtypeStruct(pairs[0].shape[1:], pairs[0].dtype)
    return pl.pallas_call(
        narrow_kernel,
        out_shape=(block,) * CORE,
        in_specs=[SMEM] + [VMEM] * X,
        out_specs=(VMEM,) * CORE,
        cost_estimate=pl.CostEstimate(flops=0, transcendentals=0, bytes_accessed=2**18),
        name="narrow",
    )(index, *pairs)


def exchange(block, to_x, to_core):
    pairs = spread(to_x, lax.all_gather(block, "z"))
    pairs = [pairs[0]] + [
        lax.ppermute(pairs[k], "x", [(i, (i + k) % X) for i in range(X)]) for k in range(1, X)
    ]
    stay, leave = narrow(to_core, pairs)
    return stay, lax.ppermute(leave, "core", [(0, 1), (1, 0)])


def local(queries, keys, values, upstream, lengths, guests, advantage, partner):
    rows = queries.shape[0]

    def by_head(array):
        return array.reshape(array.shape[0], KV_HEADS, -1).transpose(1, 0, 2)

    def swap(array):
        return lax.all_to_all(array, "head", split_axis=0, concat_axis=0, tiled=True)

    x, z, core = (lax.axis_index(name) for name in TREES)
    head = lax.axis_index("head")
    member = jnp.arange(X * CORE)
    to_x = partner[((x + member // CORE) % X * Z + z) * CORE + member % CORE] // CORE % Z
    cores = jnp.stack([core, 1 - core])
    mates = partner[(x * Z + z) * CORE + cores]
    to_core = jnp.concatenate([(x - mates // (Z * CORE)) % X, cores]).astype(jnp.int32)
    crossed = mates[0] % CORE != core
    ints = jnp.concatenate([lengths[0], guests[0], crossed[None]]).astype(jnp.int32)

    prompt = swap(jnp.concatenate([by_head(keys[:PROMPT]), by_head(values[:PROMPT])], axis=2))[0]
    qkv = swap(jnp.concatenate([by_head(queries), by_head(keys), by_head(values)], axis=2))
    far = exchange(prompt, to_x, to_core)
    grads, far_grad, own = attention(
        ints, advantage[0], qkv.reshape(ROWS, -1), prompt, upstream, *far
    )
    grads = swap(grads.reshape(KV_HEADS, rows, -1))
    stay, cross = exchange(far_grad, to_x, to_core)
    first = (own + jnp.where(crossed, cross, stay).astype(jnp.float32)).astype(jnp.bfloat16)
    first, grads = lax.optimization_barrier((first, grads))
    first = swap(jnp.broadcast_to(first[None], (KV_HEADS, PROMPT, KV)))

    def by_row(array):
        return array.transpose(1, 0, 2).reshape(array.shape[1], -1)

    def finish(lanes):
        main = by_row(grads[:, :, Q:][:, :, lanes])
        top = jnp.where(head == 0, by_row(first[:, :, lanes]), main[:PROMPT])
        return jnp.concatenate([top, main[PROMPT:]], axis=0)

    return (
        by_row(grads[:, :, :Q]),
        finish(slice(0, HEAD_DIM)),
        finish(slice(HEAD_DIM, KV)),
    )


def solution(mesh):
    mesh = Mesh(mesh.devices.reshape(X, Z, CORE, KV_HEADS), TREES + ("head",))
    tokens = P(TREES + ("head",), None)
    trees = P(TREES, None)
    return jax.shard_map(
        local,
        mesh=mesh,
        in_specs=(tokens, tokens, tokens, P(TREES, "head"), trees, trees, trees, P()),
        out_specs=(tokens, tokens, tokens),
        check_vma=False,
    )
```

time: 201 us -> 165 us (0.82)
  the two profiles are of different devices: /device:TPU:65 before, /device:TPU:1 now
where the time goes in v2:
time: 165 us; the launch traced here: 163 us
  starting transfers between devices  64.2 us (39%)
  blocking collectives  49.4 us (30%)
  waiting for transfers between devices  21.4 us (13%)
  Pallas kernels  13.2 us (8%)
  local copies, waits for them, and re-layouts  7.68 us (5%)
  other arithmetic  6.24 us (4%)
    all_gather x2, blocking collectives, exchange(): pairs = spread(to_x, lax.all_gather(block, 'z'))  49.4 us
    all_to_all x4, starting transfers between devices, swap(): lax.all_to_all(array, 'head', split_axis=0, concat_axis=0, tiled=True)  25.1 us
    ppermute x6, starting transfers between devices, exchange(): lax.ppermute(pairs[k], 'x', [(i, (i + k) % X) for i in range(X)])  20 us
    ppermute x2, starting transfers between devices, exchange(): return (stay, lax.ppermute(leave, 'core', [(0, 1), (1, 0)]))  19.1 us
    all_to_all x4, waiting for transfers between devices, swap(): lax.all_to_all(array, 'head', split_axis=0, concat_axis=0, tiled=True)  15.4 us
    pallas_call x1, Pallas kernels, attention(): pl.pallas_call(attention_kernel, out_shape=(jax.ShapeDtypeStruct((ROWS, Q...  6.8 us
    ppermute x6, waiting for transfers between devices, exchange(): lax.ppermute(pairs[k], 'x', [(i, (i + k) % X) for i in range(X)])  4.53 us
    pallas_call x2, Pallas kernels, spread(): pl.pallas_call(spread_kernel, out_shape=(pair,) * X, in_specs=[SMEM, VMEM...  3.31 us
  transfers between devices with their start and end apart: 12, of which 6 were waited for; matrix products, arithmetic and copies ran while one was open for 4% of the time, Pallas kernels for 4%

profile of v2, /device:TPU:1, one launch (start us, length us, event | category | flops | bytes accessed | tf_op | source)
XLA Modules:
  0.0 163.2 jit_solution(10860226945118379090)
XLA Ops:
  0.6 0.0 copy-start
  0.6 0.0 copy-start.2
  0.7 0.0 copy-start.3
  0.7 0.0 copy-start.4
  0.7 1.1 bitcast_bitcast_fusion.3
  1.8 0.7 pad_maximum_fusion.3
  2.5 7.6 %all-to-all-start.1 = ((bf16[8,48,256]{2,1,0:T(8,128)(2,1)}), bf16[8,48,256]{2,1,0:T(8,128)(2,1)S(1)}, u32[]{:S(2)}, u32[]{:S(2)}) async-start(bf16[8,48,256]{2,1,0:T(8,128)(2,1)} %pad_maximum_fusion.3), calls=%async_computation.1 | async-start | bytes 393216 | tf_op jit(solution)/shard_map/all_to_all | solution.py:184
  10.1 0.1 copy.58
  10.2 0.1 bitcast_bitcast_fusion.1
  10.4 1.3 pad_maximum_fusion
  11.7 7.1 %all-to-all-done.1 = bf16[8,48,256]{2,1,0:T(8,128)(2,1)S(1)} async-done(((bf16[8,48,256]{2,1,0:T(8,128)(2,1)}), bf16[8,48,256]{2,1,0:T(8,128)(2,1)S(1)}, u32[]{:S(2)}, u32[]{:S(2)}) %all-to-all-start.1) | async-done | bytes 196640 | tf_op jit(solution)/shard_map/all_to_all | solution.py:184
  18.7 3.6 %all-to-all-start = ((bf16[8,128,768]{2,1,0:T(8,128)(2,1)}), bf16[8,128,768]{2,1,0:T(8,128)(2,1)S(1)}, u32[]{:S(2)}, u32[]{:S(2)}) async-start(bf16[8,128,768]{2,1,0:T(8,128)(2,1)} %pad_maximum_fusion), calls=%async_computation | async-start | bytes 3145728 | tf_op jit(solution)/shard_map/all_to_all | solution.py:184
  22.3 0.0 copy-start.13
  22.3 0.0 copy-start.14
  22.4 0.1 fusion.10
  22.5 0.6 gather_fusion
  23.1 0.6 gather_fusion.1
  23.8 0.6 and_select_fusion.index
  24.4 0.6 fusion.11
  25.0 31.0 %all_gather.9.blocks = bf16[12,48,256]{2,1,0:T(8,128)(2,1)} all-gather(bf16[1,48,256]{2,1,0:T(8,128)(2,1)S(1)} %get-tuple-element.41), channel_id=1, replica_groups=mesh['x'=4,'z'=12,'core'=2,'head'=8] {'z'}, dimensions={0}, use_global_device_ids=true | all-gather | bytes 319488 | tf_op jit(solution)/shard_map/all_gather | solution.py:169
  56.0 1.7 %spread.2 = (bf16[2,48,256]{2,1,0:T(8,128)(2,1)}, bf16[2,48,256]{2,1,0:T(8,128)(2,1)}, bf16[2,48,256]{2,1,0:T(8,128)(2,1)}, bf16[2,48,256]{2,1,0:T(8,128)(2,1)}) custom-call(s32[8]{0:T(128)} %and_select_fusion.index, bf16[12,48,256]{2,1,0:T(8,128)(2,1)} %all_gather.9.blocks), custom_call_target="tpu_custom_call" | custom-call | bytes 524288 | tf_op jit(solution)/shard_map/spread/pallas_call | solution.py:136
  57.6 3.3 %collective-permute-start = (bf16[2,48,256]{2,1,0:T(8,128)(2,1)}, bf16[2,48,256]{2,1,0:T(8,128)(2,1)S(1)}, u32[]{:S(2)}, u32[]{:S(2)}) collective-permute-start(bf16[2,48,256]{2,1,0:T(8,128)(2,1)} %get-tuple-element.21), channel_id=1, source_target_pairs={{0,192},{192,384},{384,576},{576,0},{1,193},{193,385},{385,577},{5... | collective-permute-start | bytes 147464 | tf_op jit(solution)/shard_map/ppermute | solution.py:171
  61.0 4.4 %collective-permute-start.1 = (bf16[2,48,256]{2,1,0:T(8,128)(2,1)}, bf16[2,48,256]{2,1,0:T(8,128)(2,1)S(1)}, u32[]{:S(2)}, u32[]{:S(2)}) collective-permute-start(bf16[2,48,256]{2,1,0:T(8,128)(2,1)} %get-tuple-element.22), channel_id=1, source_target_pairs={{0,384},{192,576},{384,0},{576,192},{1,385},{193,577},{385,1},{577... | collective-permute-start | bytes 147464 | tf_op jit(solution)/shard_map/ppermute | solution.py:171
  65.3 3.1 %collective-permute-start.2 = (bf16[2,48,256]{2,1,0:T(8,128)(2,1)}, bf16[2,48,256]{2,1,0:T(8,128)(2,1)S(1)}, u32[]{:S(2)}, u32[]{:S(2)}) collective-permute-start(bf16[2,48,256]{2,1,0:T(8,128)(2,1)} %get-tuple-element.23), channel_id=1, source_target_pairs={{0,576},{192,0},{384,192},{576,384},{1,577},{193,1},{385,193},{577... | collective-permute-start | bytes 147464 | tf_op jit(solution)/shard_map/ppermute | solution.py:171
  68.4 0.7 pad_add_fusion.1.index
  69.2 0.0 collective-permute-done.refs_1_
  69.2 0.0 copy-start.6
  69.2 0.0 collective-permute-done.1.refs_2_
  69.2 0.0 copy-start.7
  69.2 1.1 collective-permute-done.2.refs_3_
  70.4 0.6 copy-done.8
  71.0 1.6 narrow.2
  72.5 10.7 %collective-permute-start.3 = (bf16[48,256]{1,0:T(8,128)(2,1)}, bf16[48,256]{1,0:T(8,128)(2,1)S(1)}, u32[]{:S(2)}, u32[]{:S(2)}) collective-permute-start(bf16[48,256]{1,0:T(8,128)(2,1)} %get-tuple-element.25), channel_id=1, source_target_pairs={{0,8},{8,0},{1,9},{9,1},{2,10},{10,2},{3,11},{11,3},{4,12},{12,4},... | collective-permute-start | bytes 73736 | tf_op jit(solution)/shard_map/ppermute | solution.py:174
  83.3 0.6 pad_add_fusion.ints
  83.9 0.4 collective-permute-done.3.cross
  84.3 0.0 all-to-all-done
  84.3 0.6 copy-done.15
  84.9 0.6 copy-done.1
  85.5 6.8 %attention.1 = (bf16[1024,768]{1,0:T(8,128)(2,1)}, bf16[48,256]{1,0:T(8,128)(2,1)}, f32[48,256]{1,0:T(8,128)}) custom-call(s32[17]{0:T(128)} %pad_add_fusion.ints, f32[8]{0:T(128)} %bitcast.103, bf16[1024,768]{1,0:T(8,128)(2,1)} %bitcast.91, bf16[48,256]{1,0:T(8,128)(2,1)} %get-tuple-element.42.prompt, bf16[1024,512]{1,0:T(8,128)(2,1)} %cot_ref.1, ...), custom_call_target="tpu_custom_call" | custom-call | flops 1000000000 | bytes 5242880 | tf_op jit(solution)/shard_map/attention/pallas_call | solution.py:110
  92.3 6.9 %all-to-all-start.2 = ((bf16[8,128,768]{2,1,0:T(8,128)(2,1)}), bf16[8,128,768]{2,1,0:T(8,128)(2,1)S(1)}, u32[]{:S(2)}, u32[]{:S(2)}) async-start(bf16[8,128,768]{2,1,0:T(8,128)(2,1)} %bitcast.92), calls=%async_computation.2 | async-start | bytes 3145728 | tf_op jit(solution)/shard_map/all_to_all | solution.py:184
  99.3 18.4 %all-gather = bf16[576,256]{1,0:T(8,128)(2,1)} all-gather(bf16[48,256]{1,0:T(8,128)(2,1)S(1)} %copy-done.12), channel_id=2, replica_groups=mesh['x'=4,'z'=12,'core'=2,'head'=8] {'z'}, dimensions={0}, use_global_device_ids=true | all-gather | bytes 319488 | tf_op jit(solution)/shard_map/all_gather | solution.py:169
  117.7 1.7 %spread.3 = (bf16[2,48,256]{2,1,0:T(8,128)(2,1)}, bf16[2,48,256]{2,1,0:T(8,128)(2,1)}, bf16[2,48,256]{2,1,0:T(8,128)(2,1)}, bf16[2,48,256]{2,1,0:T(8,128)(2,1)}) custom-call(s32[8]{0:T(128)} %and_select_fusion.index, bf16[12,48,256]{2,1,0:T(8,128)(2,1)} %bitcast.93), custom_call_target="tpu_custom_call" | custom-call | bytes 524288 | tf_op jit(solution)/shard_map/spread/pallas_call | solution.py:136
  119.3 1.9 %collective-permute-start.4 = (bf16[2,48,256]{2,1,0:T(8,128)(2,1)}, bf16[2,48,256]{2,1,0:T(8,128)(2,1)S(1)}, u32[]{:S(2)}, u32[]{:S(2)}) collective-permute-start(bf16[2,48,256]{2,1,0:T(8,128)(2,1)} %get-tuple-element.29), channel_id=1, source_target_pairs={{0,192},{192,384},{384,576},{576,0},{1,193},{193,385},{385,577},{5... | collective-permute-start | bytes 147464 | tf_op jit(solution)/shard_map/ppermute | solution.py:171
  121.2 5.4 %collective-permute-start.5 = (bf16[2,48,256]{2,1,0:T(8,128)(2,1)}, bf16[2,48,256]{2,1,0:T(8,128)(2,1)S(1)}, u32[]{:S(2)}, u32[]{:S(2)}) collective-permute-start(bf16[2,48,256]{2,1,0:T(8,128)(2,1)} %get-tuple-element.30), channel_id=1, source_target_pairs={{0,384},{192,576},{384,0},{576,192},{1,385},{193,577},{385,1},{577... | collective-permute-start | bytes 147464 | tf_op jit(solution)/shard_map/ppermute | solution.py:171
  126.7 1.9 %collective-permute-start.6 = (bf16[2,48,256]{2,1,0:T(8,128)(2,1)}, bf16[2,48,256]{2,1,0:T(8,128)(2,1)S(1)}, u32[]{:S(2)}, u32[]{:S(2)}) collective-permute-start(bf16[2,48,256]{2,1,0:T(8,128)(2,1)} %get-tuple-element.31), channel_id=1, source_target_pairs={{0,576},{192,0},{384,192},{576,384},{1,577},{193,1},{385,193},{577... | collective-permute-start | bytes 147464 | tf_op jit(solution)/shard_map/ppermute | solution.py:171
  128.6 0.0 collective-permute-done.4.refs_1_
  128.6 0.0 copy-start.9
  128.6 0.0 collective-permute-done.5.refs_2_
  128.6 3.4 %collective-permute-done.6.refs_3_ = bf16[2,48,256]{2,1,0:T(8,128)(2,1)S(1)} collective-permute-done((bf16[2,48,256]{2,1,0:T(8,128)(2,1)}, bf16[2,48,256]{2,1,0:T(8,128)(2,1)S(1)}, u32[]{:S(2)}, u32[]{:S(2)}) %collective-permute-start.6) | collective-permute-done | bytes 49184 | tf_op jit(solution)/shard_map/ppermute | solution.py:171
  132.0 0.0 copy-done.9
  132.0 0.6 copy-done.11
  132.6 1.6 narrow.3
  134.2 8.4 %collective-permute-start.7 = (bf16[48,256]{1,0:T(8,128)(2,1)}, bf16[48,256]{1,0:T(8,128)(2,1)S(1)}, u32[]{:S(2)}, u32[]{:S(2)}) collective-permute-start(bf16[48,256]{1,0:T(8,128)(2,1)} %get-tuple-element.32), channel_id=1, source_target_pairs={{0,8},{8,0},{1,9},{9,1},{2,10},{10,2},{3,11},{11,3},{4,12},{12,4},... | collective-permute-start | bytes 73736 | tf_op jit(solution)/shard_map/ppermute | solution.py:174
  142.6 1.0 collective-permute-done.7
  143.6 0.8 add_convert_fusion
  144.4 0.0 all-to-all-done.2
  144.4 0.1 slice_bitcast_fusion.1
  144.5 0.1 slice_bitcast_fusion
  144.6 0.7 broadcast_in_dim.2
  145.3 6.9 %all-to-all-start.3 = ((bf16[8,48,256]{2,1,0:T(8,128)(2,1)}), bf16[8,48,256]{2,1,0:T(8,128)(2,1)S(1)}, u32[]{:S(2)}, u32[]{:S(2)}) async-start(bf16[8,48,256]{2,1,0:T(8,128)(2,1)} %broadcast_in_dim.2), calls=%async_computation.3 | async-start | bytes 393216 | tf_op jit(solution)/shard_map/all_to_all | solution.py:184
  152.3 1.1 copy.44
  153.4 8.3 %all-to-all-done.3 = bf16[8,48,256]{2,1,0:T(8,128)(2,1)S(1)} async-done(((bf16[8,48,256]{2,1,0:T(8,128)(2,1)}), bf16[8,48,256]{2,1,0:T(8,128)(2,1)S(1)}, u32[]{:S(2)}, u32[]{:S(2)}) %all-to-all-start.3) | async-done | bytes 196640 | tf_op jit(solution)/shard_map/all_to_all | solution.py:184
  161.8 0.7 pad_maximum_fusion.2
  162.5 0.7 pad_maximum_fusion.1
  (27 shorter events, 0.2 us)
Async XLA Ops:
  0.6 21.8 %copy-start = (s32[96]{0:T(128)S(1)}, s32[96]{0:T(128)}, u32[]{:S(2)}) copy-start(s32[96]{0:T(128)} %param.15) | copy-start | bytes 1156
  0.6 9.5 %copy-start.2 = (bf16[128,4096]{1,0:T(8,128)(2,1)S(1)}, bf16[128,4096]{1,0:T(8,128)(2,1)}, u32[]{:S(2)}) copy-start(bf16[128,4096]{1,0:T(8,128)(2,1)} %param.8) | copy-start | bytes 3145732
  0.7 9.6 %copy-start.3 = (bf16[128,1024]{1,0:T(8,128)(2,1)S(1)}, bf16[128,1024]{1,0:T(8,128)(2,1)}, u32[]{:S(2)}) copy-start(bf16[128,1024]{1,0:T(8,128)(2,1)} %param.9) | copy-start | bytes 786436
  0.7 9.6 %copy-start.4 = (bf16[128,1024]{1,0:T(8,128)(2,1)S(1)}, bf16[128,1024]{1,0:T(8,128)(2,1)}, u32[]{:S(2)}) copy-start(bf16[128,1024]{1,0:T(8,128)(2,1)} %param.10) | copy-start | bytes 786436
  2.5 16.3 %all-to-all-start.1 = ((bf16[8,48,256]{2,1,0:T(8,128)(2,1)}), bf16[8,48,256]{2,1,0:T(8,128)(2,1)S(1)}, u32[]{:S(2)}, u32[]{:S(2)}) async-start(bf16[8,48,256]{2,1,0:T(8,128)(2,1)} %pad_maximum_fusion.3), calls=%async_computation.1 | async-start | bytes 393216 | tf_op jit(solution)/shard_map/all_to_all | solution.py:184
  18.7 65.6 %all-to-all-start = ((bf16[8,128,768]{2,1,0:T(8,128)(2,1)}), bf16[8,128,768]{2,1,0:T(8,128)(2,1)S(1)}, u32[]{:S(2)}, u32[]{:S(2)}) async-start(bf16[8,128,768]{2,1,0:T(8,128)(2,1)} %pad_maximum_fusion), calls=%async_computation | async-start | bytes 3145728 | tf_op jit(solution)/shard_map/all_to_all | solution.py:184
  22.3 61.0 %copy-start.13 = (s32[1,8]{1,0:T(1,128)S(1)}, s32[1,8]{1,0:T(1,128)}, u32[]{:S(2)}) copy-start(s32[1,8]{1,0:T(1,128)} %param.13) | copy-start | bytes 100
  22.3 61.0 %copy-start.14 = (s32[1,8]{1,0:T(1,128)S(1)}, s32[1,8]{1,0:T(1,128)}, u32[]{:S(2)}) copy-start(s32[1,8]{1,0:T(1,128)} %param.12) | copy-start | bytes 100
  57.6 11.5 %collective-permute-start = (bf16[2,48,256]{2,1,0:T(8,128)(2,1)}, bf16[2,48,256]{2,1,0:T(8,128)(2,1)S(1)}, u32[]{:S(2)}, u32[]{:S(2)}) collective-permute-start(bf16[2,48,256]{2,1,0:T(8,128)(2,1)} %get-tuple-element.21), channel_id=1, source_target_pairs={{0,192},{192,384},{384,576},{576,0},{1,193},{193,385},{385,577},{5... | collective-permute-start | bytes 147464 | tf_op jit(solution)/shard_map/ppermute | solution.py:171
  61.0 8.2 %collective-permute-start.1 = (bf16[2,48,256]{2,1,0:T(8,128)(2,1)}, bf16[2,48,256]{2,1,0:T(8,128)(2,1)S(1)}, u32[]{:S(2)}, u32[]{:S(2)}) collective-permute-start(bf16[2,48,256]{2,1,0:T(8,128)(2,1)} %get-tuple-element.22), channel_id=1, source_target_pairs={{0,384},{192,576},{384,0},{576,192},{1,385},{193,577},{385,1},{577... | collective-permute-start | bytes 147464 | tf_op jit(solution)/shard_map/ppermute | solution.py:171
  65.3 5.0 %collective-permute-start.2 = (bf16[2,48,256]{2,1,0:T(8,128)(2,1)}, bf16[2,48,256]{2,1,0:T(8,128)(2,1)S(1)}, u32[]{:S(2)}, u32[]{:S(2)}) collective-permute-start(bf16[2,48,256]{2,1,0:T(8,128)(2,1)} %get-tuple-element.23), channel_id=1, source_target_pairs={{0,576},{192,0},{384,192},{576,384},{1,577},{193,1},{385,193},{577... | collective-permute-start | bytes 147464 | tf_op jit(solution)/shard_map/ppermute | solution.py:171
  69.2 1.2 copy-start.6
  69.2 1.2 copy-start.7
  70.4 0.6 copy-start.8
  72.5 11.8 %collective-permute-start.3 = (bf16[48,256]{1,0:T(8,128)(2,1)}, bf16[48,256]{1,0:T(8,128)(2,1)S(1)}, u32[]{:S(2)}, u32[]{:S(2)}) collective-permute-start(bf16[48,256]{1,0:T(8,128)(2,1)} %get-tuple-element.25), channel_id=1, source_target_pairs={{0,8},{8,0},{1,9},{9,1},{2,10},{10,2},{3,11},{11,3},{4,12},{12,4},... | collective-permute-start | bytes 73736 | tf_op jit(solution)/shard_map/ppermute | solution.py:174
  84.3 0.6 copy-start.15
  84.3 1.2 copy-start.1
  92.3 7.0 %copy-start.12 = (bf16[48,256]{1,0:T(8,128)(2,1)S(1)}, bf16[48,256]{1,0:T(8,128)(2,1)}, u32[]{:S(2)}) copy-start(bf16[48,256]{1,0:T(8,128)(2,1)} %get-tuple-element.27) | copy-start | bytes 73732
  92.3 51.3 %copy-start.5 = (f32[48,256]{1,0:T(8,128)S(1)}, f32[48,256]{1,0:T(8,128)}, u32[]{:S(2)}) copy-start(f32[48,256]{1,0:T(8,128)} %get-tuple-element.26) | copy-start | bytes 147460
  92.3 52.1 %all-to-all-start.2 = ((bf16[8,128,768]{2,1,0:T(8,128)(2,1)}), bf16[8,128,768]{2,1,0:T(8,128)(2,1)S(1)}, u32[]{:S(2)}, u32[]{:S(2)}) async-start(bf16[8,128,768]{2,1,0:T(8,128)(2,1)} %bitcast.92), calls=%async_computation.2 | async-start | bytes 3145728 | tf_op jit(solution)/shard_map/all_to_all | solution.py:184
  119.3 9.3 %collective-permute-start.4 = (bf16[2,48,256]{2,1,0:T(8,128)(2,1)}, bf16[2,48,256]{2,1,0:T(8,128)(2,1)S(1)}, u32[]{:S(2)}, u32[]{:S(2)}) collective-permute-start(bf16[2,48,256]{2,1,0:T(8,128)(2,1)} %get-tuple-element.29), channel_id=1, source_target_pairs={{0,192},{192,384},{384,576},{576,0},{1,193},{193,385},{385,577},{5... | collective-permute-start | bytes 147464 | tf_op jit(solution)/shard_map/ppermute | solution.py:171
  121.2 7.4 %collective-permute-start.5 = (bf16[2,48,256]{2,1,0:T(8,128)(2,1)}, bf16[2,48,256]{2,1,0:T(8,128)(2,1)S(1)}, u32[]{:S(2)}, u32[]{:S(2)}) collective-permute-start(bf16[2,48,256]{2,1,0:T(8,128)(2,1)} %get-tuple-element.30), channel_id=1, source_target_pairs={{0,384},{192,576},{384,0},{576,192},{1,385},{193,577},{385,1},{577... | collective-permute-start | bytes 147464 | tf_op jit(solution)/shard_map/ppermute | solution.py:171
  126.7 5.3 %collective-permute-start.6 = (bf16[2,48,256]{2,1,0:T(8,128)(2,1)}, bf16[2,48,256]{2,1,0:T(8,128)(2,1)S(1)}, u32[]{:S(2)}, u32[]{:S(2)}) collective-permute-start(bf16[2,48,256]{2,1,0:T(8,128)(2,1)} %get-tuple-element.31), channel_id=1, source_target_pairs={{0,576},{192,0},{384,192},{576,384},{1,577},{193,1},{385,193},{577... | collective-permute-start | bytes 147464 | tf_op jit(solution)/shard_map/ppermute | solution.py:171
  128.6 3.4 %copy-start.9 = (bf16[2,48,256]{2,1,0:T(8,128)(2,1)}, bf16[2,48,256]{2,1,0:T(8,128)(2,1)S(1)}, u32[]{:S(2)}) copy-start(bf16[2,48,256]{2,1,0:T(8,128)(2,1)S(1)} %collective-permute-done.4.refs_1_) | copy-start | bytes 147460
  128.6 3.4 %copy-start.10 = (bf16[2,48,256]{2,1,0:T(8,128)(2,1)}, bf16[2,48,256]{2,1,0:T(8,128)(2,1)S(1)}, u32[]{:S(2)}) copy-start(bf16[2,48,256]{2,1,0:T(8,128)(2,1)S(1)} %collective-permute-done.5.refs_2_) | copy-start | bytes 147460
  132.0 0.6 copy-start.11
  134.2 9.4 %collective-permute-start.7 = (bf16[48,256]{1,0:T(8,128)(2,1)}, bf16[48,256]{1,0:T(8,128)(2,1)S(1)}, u32[]{:S(2)}, u32[]{:S(2)}) collective-permute-start(bf16[48,256]{1,0:T(8,128)(2,1)} %get-tuple-element.32), channel_id=1, source_target_pairs={{0,8},{8,0},{1,9},{9,1},{2,10},{10,2},{3,11},{11,3},{4,12},{12,4},... | collective-permute-start | bytes 73736 | tf_op jit(solution)/shard_map/ppermute | solution.py:174
  145.3 16.4 %all-to-all-start.3 = ((bf16[8,48,256]{2,1,0:T(8,128)(2,1)}), bf16[8,48,256]{2,1,0:T(8,128)(2,1)S(1)}, u32[]{:S(2)}, u32[]{:S(2)}) async-start(bf16[8,48,256]{2,1,0:T(8,128)(2,1)} %broadcast_in_dim.2), calls=%async_computation.3 | async-start | bytes 393216 | tf_op jit(solution)/shard_map/all_to_all | solution.py:184

commit v3 on v2

v3 whole, which is shorter than its diff:
```python
import jax
import jax.numpy as jnp
from jax import lax
from jax.experimental import pallas as pl
from jax.experimental.pallas import tpu as pltpu
from jax.sharding import Mesh, PartitionSpec as P

HEAD_DIM = 128
PROMPT = 48
RESP = 8
RESP_LEN = 122
ROWS = 1024
GROUP = 4
KV_HEADS = 8
WINDOW = 128
Q = GROUP * HEAD_DIM
KV = 2 * HEAD_DIM
TREES = ("x", "z", "core")
PLANE = ("x", "core")
X, Z, CORE = 4, 12, 2


def attend(q_rows, keys, vals, cot, allowed):
    scaling = HEAD_DIM ** (-0.5)
    nt = (((1,), (1,)), ((), ()))
    scores = lax.dot_general(keys, q_rows, nt, preferred_element_type=jnp.float32) * scaling
    scores = jnp.where(allowed, scores, -jnp.inf)
    lifted = jnp.exp(scores - jnp.max(scores, axis=0, keepdims=True))
    probs = lifted * (1.0 / jnp.sum(lifted, axis=0, keepdims=True))
    probs_low = probs.astype(jnp.bfloat16)
    grad_probs = lax.dot_general(vals, cot, nt, preferred_element_type=jnp.float32)
    inner = jnp.sum(probs_low.astype(jnp.float32) * grad_probs, axis=0, keepdims=True)
    grad_scores = (probs * (grad_probs - inner) * scaling).astype(jnp.bfloat16)
    grad_v = jnp.dot(probs_low, cot, preferred_element_type=jnp.float32)
    grad_k = jnp.dot(grad_scores, q_rows, preferred_element_type=jnp.float32)
    tn = (((0,), (0,)), ((), ()))
    grad_q = lax.dot_general(grad_scores, keys, tn, preferred_element_type=jnp.float32)
    return grad_q, jnp.concatenate([grad_k, grad_v], axis=1)


def stack_heads(block):
    return jnp.concatenate(
        [block[:, j * HEAD_DIM : (j + 1) * HEAD_DIM] for j in range(GROUP)], axis=0
    )


def unstack_heads(block, rows):
    return jnp.concatenate([block[j * rows : (j + 1) * rows] for j in range(GROUP)], axis=1)


def attention_kernel(
    partner, lengths, guests, adv, qkv, cot_ref, far_in, grads, far_out, own_out, pre, acc
):
    iota = lax.broadcasted_iota
    pre[0] = qkv[:PROMPT, Q:]
    pre[1] = far_in[partner_entry(partner)]
    acc[1] = jnp.zeros((PROMPT, KV), jnp.float32)

    wide = (PROMPT, GROUP * PROMPT)
    query = iota(jnp.int32, wide, 1)
    for j in range(1, GROUP):
        query = jnp.where(query >= PROMPT, query - PROMPT, query)
    grad_q, grad_kv = attend(
        stack_heads(qkv[:PROMPT, :Q]),
        pre[0, :, :HEAD_DIM],
        pre[0, :, HEAD_DIM:],
        stack_heads(cot_ref[:PROMPT, :]),
        iota(jnp.int32, wide, 0) <= query,
    )
    grads[:PROMPT, :Q] = unstack_heads(grad_q, PROMPT).astype(jnp.bfloat16)
    grads[:PROMPT, Q:] = jnp.zeros((PROMPT, KV), jnp.bfloat16)
    acc[0] = grad_kv

    for slot in range(RESP):
        first = PROMPT + RESP_LEN * slot
        start = first // 8 * 8
        skip = first - start
        rows = slice(start, start + WINDOW)
        guest = guests[0, slot]
        keys = jnp.concatenate([pre[guest, :, :HEAD_DIM], qkv[rows, Q : Q + HEAD_DIM]], axis=0)
        vals = jnp.concatenate([pre[guest, :, HEAD_DIM:], qkv[rows, Q + HEAD_DIM :]], axis=0)
        token = iota(jnp.int32, (WINDOW, Q), 0) - skip
        weight = jnp.where((token >= 0) & (token < lengths[0, slot]), adv[0, slot], 0.0)
        cot = (cot_ref[rows, :].astype(jnp.float32) * weight).astype(jnp.bfloat16)
        shape = (PROMPT + WINDOW, GROUP * WINDOW)
        key = iota(jnp.int32, shape, 0)
        query = iota(jnp.int32, shape, 1) & (WINDOW - 1)
        allowed = (key < PROMPT) | ((key >= PROMPT + skip) & (key - PROMPT <= query))
        grad_q, grad_kv = attend(stack_heads(qkv[rows, :Q]), keys, vals, stack_heads(cot), allowed)
        acc[guest] += grad_kv[:PROMPT]
        new = jnp.concatenate([unstack_heads(grad_q, WINDOW), grad_kv[PROMPT:]], axis=1)
        if skip:
            old = grads[start : start + 8, :].astype(jnp.float32)
            top = jnp.where(iota(jnp.int32, old.shape, 0) < skip, old, new[:8])
            new = jnp.concatenate([top, new[8:]], axis=0)
        grads[rows, :] = new.astype(jnp.bfloat16)

    own_out[...] = acc[0]
    far_out[...] = acc[1].astype(jnp.bfloat16)


VMEM = pl.BlockSpec(memory_space=pltpu.VMEM)
SMEM = pl.BlockSpec(memory_space=pltpu.SMEM)
SMALL = pltpu.CompilerParams(vmem_limit_bytes=8 * 2**20)
LARGE = pltpu.CompilerParams(vmem_limit_bytes=24 * 2**20)


def attention(partner, lengths, guests, adv, qkv, cot, far):
    return pl.pallas_call(
        attention_kernel,
        out_shape=(
            jax.ShapeDtypeStruct((ROWS, Q + KV), jnp.bfloat16),
            jax.ShapeDtypeStruct((PROMPT, KV), jnp.bfloat16),
            jax.ShapeDtypeStruct((PROMPT, KV), jnp.float32),
        ),
        in_specs=[SMEM] * 4 + [VMEM] * 3,
        out_specs=(VMEM, VMEM, VMEM),
        scratch_shapes=[
            pltpu.VMEM((2, PROMPT, KV), jnp.bfloat16),
            pltpu.VMEM((2, PROMPT, KV), jnp.float32),
        ],
        cost_estimate=pl.CostEstimate(flops=10**9, transcendentals=720896, bytes_accessed=5 * 2**20),
        compiler_params=LARGE,
        name="attention",
    )(partner, lengths, guests, adv, qkv, cot, far)


def place():
    return tuple(lax.axis_index(name) for name in TREES)


def pick_kernel(partner, blocks, out):
    _, z, core = place()
    for i in range(X):
        wanted = partner[(i * Z + z) * CORE + core]
        out[i] = blocks[lax.rem(wanted, Z * CORE)]


def pick(partner, blocks):
    return pl.pallas_call(
        pick_kernel,
        out_shape=jax.ShapeDtypeStruct((X,) + blocks.shape[1:], blocks.dtype),
        in_specs=[SMEM, VMEM],
        out_specs=VMEM,
        cost_estimate=pl.CostEstimate(flops=0, transcendentals=0, bytes_accessed=2**18),
        compiler_params=SMALL,
        name="pick",
    )(partner, blocks)


def exchange(block, partner):
    wanted = pick(partner, lax.all_gather(block, ("z", "core")))
    return lax.all_gather(wanted, "x", axis=0, tiled=True)


def partner_entry(partner):
    x, z, core = place()
    return X * lax.div(partner[(x * Z + z) * CORE + core], Z * CORE) + x


def lay_out_kernel(keys, values, out):
    for i in range(KV_HEADS):
        lanes = slice(i * HEAD_DIM, (i + 1) * HEAD_DIM)
        out[i, :, :HEAD_DIM] = keys[:, lanes]
        out[i, :, HEAD_DIM:] = values[:, lanes]


def lay_out(keys, values):
    rows = pl.BlockSpec((PROMPT, KV_HEADS * HEAD_DIM), lambda i: (0, 0))
    return pl.pallas_call(
        lay_out_kernel,
        grid=(1,),
        out_shape=jax.ShapeDtypeStruct((KV_HEADS, PROMPT, KV), jnp.bfloat16),
        in_specs=[rows, rows],
        out_specs=pl.BlockSpec((KV_HEADS, PROMPT, KV), lambda i: (0, 0, 0)),
        cost_estimate=pl.CostEstimate(flops=0, transcendentals=0, bytes_accessed=2**19),
        compiler_params=SMALL,
        name="lay_out",
    )(keys, values)


def by_token_kernel(main, first, grad_k, grad_v):
    owner = lax.axis_index("head") == 0
    for i in range(KV_HEADS):
        lanes = slice(i * HEAD_DIM, (i + 1) * HEAD_DIM)
        for ref, start in ((grad_k, 0), (grad_v, HEAD_DIM)):
            part = slice(start, start + HEAD_DIM)
            old = main[i, :PROMPT, part].astype(jnp.float32)
            top = jnp.where(owner, first[i, :, part].astype(jnp.float32), old)
            ref[:PROMPT, lanes] = top.astype(ref.dtype)
            ref[PROMPT:, lanes] = main[i, PROMPT:, part]


def by_token(grads, first):
    rows = grads.shape[1]
    out = jax.ShapeDtypeStruct((rows, KV_HEADS * HEAD_DIM), jnp.bfloat16)
    whole = pl.BlockSpec(out.shape, lambda i: (0, 0))
    return pl.pallas_call(
        by_token_kernel,
        grid=(1,),
        out_shape=(out, out),
        in_specs=[
            pl.BlockSpec((KV_HEADS, rows, KV), lambda i: (0, 0, Q // KV)),
            pl.BlockSpec((KV_HEADS, PROMPT, KV), lambda i: (0, 0, 0)),
        ],
        out_specs=(whole, whole),
        cost_estimate=pl.CostEstimate(flops=0, transcendentals=0, bytes_accessed=2**20),
        compiler_params=SMALL,
        name="by_token",
    )(grads, first)


def finish_kernel(partner, own, back, out):
    block = own[...] + back[partner_entry(partner)].astype(jnp.float32)
    for i in range(KV_HEADS):
        out[i] = block.astype(out.dtype)


def finish(partner, own, back):
    return pl.pallas_call(
        finish_kernel,
        out_shape=jax.ShapeDtypeStruct((KV_HEADS,) + own.shape, jnp.bfloat16),
        in_specs=[SMEM, VMEM, VMEM],
        out_specs=VMEM,
        cost_estimate=pl.CostEstimate(flops=0, transcendentals=0, bytes_accessed=2**18),
        compiler_params=SMALL,
        name="finish",
    )(partner, own, back)


def local(queries, keys, values, upstream, lengths, guests, advantage, partner):
    rows = queries.shape[0]

    def by_head(array):
        return array.reshape(array.shape[0], KV_HEADS, -1).transpose(1, 0, 2)

    def swap(array):
        return lax.all_to_all(array, "head", split_axis=0, concat_axis=0, tiled=True)

    prompt = swap(lay_out(keys, values))
    qkv = swap(jnp.concatenate([by_head(queries), by_head(keys), by_head(values)], axis=2))
    far = exchange(prompt[0], partner)
    grads, far_grad, own = attention(
        partner, lengths, guests, advantage, qkv.reshape(ROWS, -1), upstream, far
    )
    grads = swap(grads.reshape(KV_HEADS, rows, -1))
    first = finish(partner, own, exchange(far_grad, partner))
    first, grads = lax.optimization_barrier((first, grads))
    first = swap(first)
    grad_q = grads[:, :, :Q].transpose(1, 0, 2).reshape(rows, -1)
    return (grad_q,) + tuple(by_token(grads, first))


def solution(mesh):
    mesh = Mesh(mesh.devices.reshape(X, Z, CORE, KV_HEADS), TREES + ("head",))
    tokens = P(TREES + ("head",), None)
    trees = P(TREES, None)
    return jax.shard_map(
        local,
        mesh=mesh,
        in_specs=(tokens, tokens, tokens, P(TREES, "head"), trees, trees, trees, P()),
        out_specs=(tokens, tokens, tokens),
        check_vma=False,
    )
```

time: 165 us -> 141 us (0.85)
  the two profiles are of different devices: /device:TPU:1 before, /device:TPU:2 now
where the time goes in v3:
time: 141 us; the launch traced here: 140 us
  blocking collectives  82.7 us (59%)
  starting transfers between devices  24.4 us (17%)
  waiting for transfers between devices  14 us (10%)
  Pallas kernels  9.71 us (7%)
  local copies, waits for them, and re-layouts  7.37 us (5%)
    all_gather x2, blocking collectives, exchange(): wanted = pick(partner, lax.all_gather(block, ('z', 'core')))  57 us
    all_gather x2, blocking collectives, exchange(): return lax.all_gather(wanted, 'x', axis=0, tiled=True)  25.7 us
    all_to_all x4, starting transfers between devices, swap(): lax.all_to_all(array, 'head', split_axis=0, concat_axis=0, tiled=True)  24.4 us
    all_to_all x4, waiting for transfers between devices, swap(): lax.all_to_all(array, 'head', split_axis=0, concat_axis=0, tiled=True)  14 us
    pallas_call x1, Pallas kernels, attention(): pl.pallas_call(attention_kernel, out_shape=(jax.ShapeDtypeStruct((ROWS, Q...  5.64 us
    unnamed x19, local copies, waits for them, and re-layouts  3.24 us
  transfers between devices with their start and end apart: 4, of which 3 were waited for; matrix products, arithmetic and copies ran while one was open for 5% of the time, Pallas kernels for 2%

profile of v3, /device:TPU:2, one launch (start us, length us, event | category | flops | bytes accessed | tf_op | source)
XLA Modules:
  0.0 140.2 jit_solution(3876100683985274193)
XLA Ops:
  0.6 0.0 copy-start
  0.6 0.9 copy-done
  1.6 0.0 copy-start.2
  1.6 0.9 copy-done.2
  2.5 0.0 copy-start.1
  2.5 0.0 copy-start.3
  2.5 0.7 lay_out.1
  3.2 7.1 %all-to-all-start.1 = ((bf16[8,48,256]{2,1,0:T(8,128)(2,1)}), bf16[8,48,256]{2,1,0:T(8,128)(2,1)S(1)}, u32[]{:S(2)}, u32[]{:S(2)}) async-start(bf16[8,48,256]{2,1,0:T(8,128)(2,1)} %lay_out.1), calls=%async_computation.1 | async-start | bytes 393216 | tf_op jit(solution)/shard_map/all_to_all | solution.py:238
  10.3 1.3 copy.30
  11.7 0.0 copy-done.1
  11.7 0.0 copy-done.3
  11.7 0.1 bitcast_bitcast_fusion.1
  11.8 1.3 pad_maximum_fusion
  13.1 0.0 copy-start.4
  13.1 7.7 %all-to-all-done.1 = bf16[8,48,256]{2,1,0:T(8,128)(2,1)S(1)} async-done(((bf16[8,48,256]{2,1,0:T(8,128)(2,1)}), bf16[8,48,256]{2,1,0:T(8,128)(2,1)S(1)}, u32[]{:S(2)}, u32[]{:S(2)}) %all-to-all-start.1) | async-done | bytes 196640 | tf_op jit(solution)/shard_map/all_to_all | solution.py:238
  20.8 3.6 %all-to-all-start = ((bf16[8,128,768]{2,1,0:T(8,128)(2,1)}), bf16[8,128,768]{2,1,0:T(8,128)(2,1)S(1)}, u32[]{:S(2)}, u32[]{:S(2)}) async-start(bf16[8,128,768]{2,1,0:T(8,128)(2,1)} %pad_maximum_fusion), calls=%async_computation | async-start | bytes 3145728 | tf_op jit(solution)/shard_map/all_to_all | solution.py:238
  24.4 0.0 copy-start.5
  24.4 0.0 copy-start.6
  24.4 0.0 copy-start.7
  24.4 0.0 copy-start.8
  24.5 34.8 %all_gather.15.blocks = bf16[24,48,256]{2,1,0:T(8,128)(2,1)S(1)} all-gather(bf16[1,48,256]{2,1,0:T(8,128)(2,1)S(1)} %slice.8), channel_id=1, replica_groups=mesh['x'=4,'z'=12,'core'=2,'head'=8] {'z','core'}, dimensions={0}, use_global_device_ids=true | all-gather | bytes 614400 | tf_op jit(solution)/shard_map/all_gather | solution.py:152
  59.3 0.0 copy-done.4
  59.3 0.6 pick.2
  59.9 13.0 %all_gather.16.far_in = bf16[16,48,256]{2,1,0:T(8,128)(2,1)S(1)} all-gather(bf16[4,48,256]{2,1,0:T(8,128)(2,1)S(1)} %pick.2), channel_id=1, replica_groups=mesh['x'=4,'z'=12,'core'=2,'head'=8] {'x'}, dimensions={0}, use_global_device_ids=true | all-gather | bytes 491520 | tf_op jit(solution)/shard_map/all_gather | solution.py:153
  72.9 0.0 all-to-all-done
  72.9 0.0 copy-done.5
  72.9 0.0 copy-done.6
  72.9 0.0 copy-done.7
  72.9 0.0 copy-done.8
  72.9 5.6 %attention.1 = (bf16[1024,768]{1,0:T(8,128)(2,1)}, bf16[48,256]{1,0:T(8,128)(2,1)S(1)}, f32[48,256]{1,0:T(8,128)S(1)}) custom-call(s32[96]{0:T(128)S(1)} %copy-done.4, s32[1,8]{1,0:T(1,128)S(1)} %copy-done.6, s32[1,8]{1,0:T(1,128)S(1)} %copy-done.7, f32[1,8]{1,0:T(1,128)S(1)} %copy-done.8, bf16[1024,768]{1,0:T(8,128)(2,1)S(1)} %bitcast.28, ...), custom_call_target="tpu_custom_call" | custom-call | flops 1000000000 | bytes 5242880 | tf_op jit(solution)/shard_map/attention/pallas_call | solution.py:109
  78.5 7.1 %all-to-all-start.2 = ((bf16[8,128,768]{2,1,0:T(8,128)(2,1)}), bf16[8,128,768]{2,1,0:T(8,128)(2,1)S(1)}, u32[]{:S(2)}, u32[]{:S(2)}) async-start(bf16[8,128,768]{2,1,0:T(8,128)(2,1)} %bitcast.5), calls=%async_computation.2 | async-start | bytes 3145728 | tf_op jit(solution)/shard_map/all_to_all | solution.py:238
  85.6 22.1 %all-gather = bf16[1152,256]{1,0:T(8,128)(2,1)S(1)} all-gather(bf16[48,256]{1,0:T(8,128)(2,1)S(1)} %get-tuple-element.11), channel_id=2, replica_groups=mesh['x'=4,'z'=12,'core'=2,'head'=8] {'z','core'}, dimensions={0}, use_global_device_ids=true | all-gather | bytes 614400 | tf_op jit(solution)/shard_map/all_gather | solution.py:152
  107.8 0.6 pick.3
  108.3 12.7 %all_gather.19.back = bf16[16,48,256]{2,1,0:T(8,128)(2,1)S(1)} all-gather(bf16[4,48,256]{2,1,0:T(8,128)(2,1)S(1)} %pick.3), channel_id=1, replica_groups=mesh['x'=4,'z'=12,'core'=2,'head'=8] {'x'}, dimensions={0}, use_global_device_ids=true | all-gather | bytes 491520 | tf_op jit(solution)/shard_map/all_gather | solution.py:153
  121.1 1.3 finish.1
  122.3 0.5 all-to-all-done.2.main
  122.8 6.7 %all-to-all-start.3 = ((bf16[8,48,256]{2,1,0:T(8,128)(2,1)}), bf16[8,48,256]{2,1,0:T(8,128)(2,1)S(1)}, u32[]{:S(2)}, u32[]{:S(2)}) async-start(bf16[8,48,256]{2,1,0:T(8,128)(2,1)} %finish.1), calls=%async_computation.3 | async-start | bytes 393216 | tf_op jit(solution)/shard_map/all_to_all | solution.py:238
  129.5 1.1 slice_bitcast_fusion
  130.6 1.6 %copy.22 = bf16[128,8,512]{0,2,1:T(8,128)(2,1)S(1)} copy(bf16[128,8,512]{2,0,1:T(8,128)(2,1)} %slice_bitcast_fusion) | data formatting | bytes 2097152 | tf_op jit(solution)/shard_map/transpose | solution.py:250
  132.2 1.3 copy.23
  133.5 5.8 %all-to-all-done.3.first = bf16[8,48,256]{2,1,0:T(8,128)(2,1)S(1)} async-done(((bf16[8,48,256]{2,1,0:T(8,128)(2,1)}), bf16[8,48,256]{2,1,0:T(8,128)(2,1)S(1)}, u32[]{:S(2)}, u32[]{:S(2)}) %all-to-all-start.3) | async-done | bytes 196640 | tf_op jit(solution)/shard_map/all_to_all | solution.py:238
  139.3 0.9 by_token.1
  (1 shorter events, 0.0 us)
Async XLA Ops:
  0.6 1.0 copy-start
  1.6 0.9 copy-start.2
  2.5 9.1 %copy-start.1 = (bf16[128,1024]{1,0:T(8,128)(2,1)S(1)}, bf16[128,1024]{1,0:T(8,128)(2,1)}, u32[]{:S(2)}) copy-start(bf16[128,1024]{1,0:T(8,128)(2,1)} %keys.1) | copy-start | bytes 786436
  2.5 9.1 %copy-start.3 = (bf16[128,1024]{1,0:T(8,128)(2,1)S(1)}, bf16[128,1024]{1,0:T(8,128)(2,1)}, u32[]{:S(2)}) copy-start(bf16[128,1024]{1,0:T(8,128)(2,1)} %values.1) | copy-start | bytes 786436
  3.2 17.6 %all-to-all-start.1 = ((bf16[8,48,256]{2,1,0:T(8,128)(2,1)}), bf16[8,48,256]{2,1,0:T(8,128)(2,1)S(1)}, u32[]{:S(2)}, u32[]{:S(2)}) async-start(bf16[8,48,256]{2,1,0:T(8,128)(2,1)} %lay_out.1), calls=%async_computation.1 | async-start | bytes 393216 | tf_op jit(solution)/shard_map/all_to_all | solution.py:238
  13.1 46.2 %copy-start.4 = (s32[96]{0:T(128)S(1)}, s32[96]{0:T(128)}, u32[]{:S(2)}) copy-start(s32[96]{0:T(128)} %partner.7) | copy-start | bytes 1156
  20.8 52.1 %all-to-all-start = ((bf16[8,128,768]{2,1,0:T(8,128)(2,1)}), bf16[8,128,768]{2,1,0:T(8,128)(2,1)S(1)}, u32[]{:S(2)}, u32[]{:S(2)}) async-start(bf16[8,128,768]{2,1,0:T(8,128)(2,1)} %pad_maximum_fusion), calls=%async_computation | async-start | bytes 3145728 | tf_op jit(solution)/shard_map/all_to_all | solution.py:238
  24.4 48.5 %copy-start.5 = (bf16[1024,512]{1,0:T(8,128)(2,1)S(1)}, bf16[1024,512]{1,0:T(8,128)(2,1)}, u32[]{:S(2)}) copy-start(bf16[1024,512]{1,0:T(8,128)(2,1)} %cot_ref.1) | copy-start | bytes 3145732
  24.4 48.5 %copy-start.6 = (s32[1,8]{1,0:T(1,128)S(1)}, s32[1,8]{1,0:T(1,128)}, u32[]{:S(2)}) copy-start(s32[1,8]{1,0:T(1,128)} %lengths.1) | copy-start | bytes 100
  24.4 48.5 %copy-start.7 = (s32[1,8]{1,0:T(1,128)S(1)}, s32[1,8]{1,0:T(1,128)}, u32[]{:S(2)}) copy-start(s32[1,8]{1,0:T(1,128)} %guests.1) | copy-start | bytes 100
  24.4 48.5 %copy-start.8 = (f32[1,8]{1,0:T(1,128)S(1)}, f32[1,8]{1,0:T(1,128)}, u32[]{:S(2)}) copy-start(f32[1,8]{1,0:T(1,128)} %adv.1) | copy-start | bytes 100
  78.5 44.3 %all-to-all-start.2 = ((bf16[8,128,768]{2,1,0:T(8,128)(2,1)}), bf16[8,128,768]{2,1,0:T(8,128)(2,1)S(1)}, u32[]{:S(2)}, u32[]{:S(2)}) async-start(bf16[8,128,768]{2,1,0:T(8,128)(2,1)} %bitcast.5), calls=%async_computation.2 | async-start | bytes 3145728 | tf_op jit(solution)/shard_map/all_to_all | solution.py:238
  122.8 16.4 %all-to-all-start.3 = ((bf16[8,48,256]{2,1,0:T(8,128)(2,1)}), bf16[8,48,256]{2,1,0:T(8,128)(2,1)S(1)}, u32[]{:S(2)}, u32[]{:S(2)}) async-start(bf16[8,48,256]{2,1,0:T(8,128)(2,1)} %finish.1), calls=%async_computation.3 | async-start | bytes 393216 | tf_op jit(solution)/shard_map/all_to_all | solution.py:238

commit v4 on v3

--- a/solution.py
+++ b/solution.py
@@ -20,21 +20,27 @@
 X, Z, CORE = 4, 12, 2
 
 
-def attend(q_rows, keys, vals, cot, allowed):
-    scaling = HEAD_DIM ** (-0.5)
-    nt = (((1,), (1,)), ((), ()))
-    scores = lax.dot_general(keys, q_rows, nt, preferred_element_type=jnp.float32) * scaling
-    scores = jnp.where(allowed, scores, -jnp.inf)
-    lifted = jnp.exp(scores - jnp.max(scores, axis=0, keepdims=True))
-    probs = lifted * (1.0 / jnp.sum(lifted, axis=0, keepdims=True))
-    probs_low = probs.astype(jnp.bfloat16)
-    grad_probs = lax.dot_general(vals, cot, nt, preferred_element_type=jnp.float32)
-    inner = jnp.sum(probs_low.astype(jnp.float32) * grad_probs, axis=0, keepdims=True)
-    grad_scores = (probs * (grad_probs - inner) * scaling).astype(jnp.bfloat16)
-    grad_v = jnp.dot(probs_low, cot, preferred_element_type=jnp.float32)
+NT = (((1,), (1,)), ((), ()))
+TN = (((0,), (0,)), ((), ()))
+SCALING = HEAD_DIM ** (-0.5)
+LOG2_E = 1.4426950408889634
+
+
+def products(q_rows, keys, vals, cot):
+    scores = lax.dot_general(keys, q_rows, NT, preferred_element_type=jnp.float32)
+    grad_probs = lax.dot_general(vals, cot, NT, preferred_element_type=jnp.float32)
+    return scores * (SCALING * LOG2_E), grad_probs
+
+
+def backward(scores, grad_probs, q_rows, keys, cot):
+    lifted = jnp.exp2(scores - jnp.max(scores, axis=0, keepdims=True))
+    share = 1.0 / jnp.sum(lifted, axis=0, keepdims=True)
+    inner = jnp.sum(lifted * grad_probs, axis=0, keepdims=True) * share
+    probs = lifted * share
+    grad_scores = (probs * (grad_probs - inner) * SCALING).astype(jnp.bfloat16)
+    grad_v = jnp.dot(probs.astype(jnp.bfloat16), cot, preferred_element_type=jnp.float32)
     grad_k = jnp.dot(grad_scores, q_rows, preferred_element_type=jnp.float32)
-    tn = (((0,), (0,)), ((), ()))
-    grad_q = lax.dot_general(grad_scores, keys, tn, preferred_element_type=jnp.float32)
+    grad_q = lax.dot_general(grad_scores, keys, TN, preferred_element_type=jnp.float32)
     return grad_q, jnp.concatenate([grad_k, grad_v], axis=1)
 
 
@@ -49,52 +55,72 @@
 
 
 def attention_kernel(
-    partner, lengths, guests, adv, qkv, cot_ref, far_in, grads, far_out, own_out, pre, acc
+    partner, lengths, guests, adv, qkv, cot_ref, far_in, grads, far_out, own_out, pre, acc, later
 ):
     iota = lax.broadcasted_iota
     pre[0] = qkv[:PROMPT, Q:]
     pre[1] = far_in[partner_entry(partner)]
     acc[1] = jnp.zeros((PROMPT, KV), jnp.float32)
-
-    wide = (PROMPT, GROUP * PROMPT)
-    query = iota(jnp.int32, wide, 1)
-    for j in range(1, GROUP):
-        query = jnp.where(query >= PROMPT, query - PROMPT, query)
-    grad_q, grad_kv = attend(
-        stack_heads(qkv[:PROMPT, :Q]),
-        pre[0, :, :HEAD_DIM],
-        pre[0, :, HEAD_DIM:],
-        stack_heads(cot_ref[:PROMPT, :]),
-        iota(jnp.int32, wide, 0) <= query,
-    )
-    grads[:PROMPT, :Q] = unstack_heads(grad_q, PROMPT).astype(jnp.bfloat16)
-    grads[:PROMPT, Q:] = jnp.zeros((PROMPT, KV), jnp.bfloat16)
-    acc[0] = grad_kv
-
-    for slot in range(RESP):
+    causal = iota(jnp.int32, later.shape, 0) <= iota(jnp.int32, later.shape, 1)
+    later[...] = jnp.where(causal, 0.0, -jnp.inf)
+
+    def window(slot):
         first = PROMPT + RESP_LEN * slot
         start = first // 8 * 8
-        skip = first - start
-        rows = slice(start, start + WINDOW)
+        return slice(start, start + WINDOW), first - start
+
+    def load(slot):
+        rows, skip = window(slot)
         guest = guests[0, slot]
+        q_rows = stack_heads(qkv[rows, :Q])
         keys = jnp.concatenate([pre[guest, :, :HEAD_DIM], qkv[rows, Q : Q + HEAD_DIM]], axis=0)
         vals = jnp.concatenate([pre[guest, :, HEAD_DIM:], qkv[rows, Q + HEAD_DIM :]], axis=0)
-        token = iota(jnp.int32, (WINDOW, Q), 0) - skip
+        token = iota(jnp.int32, (WINDOW, HEAD_DIM), 0) - skip
         weight = jnp.where((token >= 0) & (token < lengths[0, slot]), adv[0, slot], 0.0)
-        cot = (cot_ref[rows, :].astype(jnp.float32) * weight).astype(jnp.bfloat16)
-        shape = (PROMPT + WINDOW, GROUP * WINDOW)
-        key = iota(jnp.int32, shape, 0)
-        query = iota(jnp.int32, shape, 1) & (WINDOW - 1)
-        allowed = (key < PROMPT) | ((key >= PROMPT + skip) & (key - PROMPT <= query))
-        grad_q, grad_kv = attend(stack_heads(qkv[rows, :Q]), keys, vals, stack_heads(cot), allowed)
-        acc[guest] += grad_kv[:PROMPT]
+        cot = jnp.concatenate(
+            [
+                (cot_ref[rows, lanes].astype(jnp.float32) * weight).astype(jnp.bfloat16)
+                for lanes in (slice(j * HEAD_DIM, (j + 1) * HEAD_DIM) for j in range(GROUP))
+            ],
+            axis=0,
+        )
+        return (q_rows, keys, cot), products(q_rows, keys, vals, cot)
+
+    def emit(slot, operands, scores, grad_probs):
+        rows, skip = window(slot)
+        bias = later[...]
+        if skip:
+            top = jnp.where(iota(jnp.int32, (8, WINDOW), 0) < skip, -jnp.inf, bias[:8])
+            bias = jnp.concatenate([top, bias[8:]], axis=0)
+        bias = jnp.concatenate([bias] * GROUP, axis=1)
+        scores = jnp.concatenate([scores[:PROMPT], scores[PROMPT:] + bias], axis=0)
+        grad_q, grad_kv = backward(scores, grad_probs, *operands)
+        acc[guests[0, slot]] += grad_kv[:PROMPT]
         new = jnp.concatenate([unstack_heads(grad_q, WINDOW), grad_kv[PROMPT:]], axis=1)
         if skip:
-            old = grads[start : start + 8, :].astype(jnp.float32)
+            old = grads[rows.start : rows.start + 8, :].astype(jnp.float32)
             top = jnp.where(iota(jnp.int32, old.shape, 0) < skip, old, new[:8])
             new = jnp.concatenate([top, new[8:]], axis=0)
         grads[rows, :] = new.astype(jnp.bfloat16)
 
+    q_rows = stack_heads(qkv[:PROMPT, :Q])
+    cot = stack_heads(cot_ref[:PROMPT, :])
+    keys = pre[0, :, :HEAD_DIM]
+    scores, grad_probs = products(q_rows, keys, pre[0, :, HEAD_DIM:], cot)
+    query = iota(jnp.int32, scores.shape, 1)
+    for j in range(1, GROUP):
+        query = jnp.where(query >= PROMPT, query - PROMPT, query)
+    scores = jnp.where(iota(jnp.int32, scores.shape, 0) <= query, scores, -jnp.inf)
+    grad_q, acc[0] = backward(scores, grad_probs, q_rows, keys, cot)
+    grads[:PROMPT, :Q] = unstack_heads(grad_q, PROMPT).astype(jnp.bfloat16)
+    grads[:PROMPT, Q:] = jnp.zeros((PROMPT, KV), jnp.bfloat16)
+
+    ahead = load(0)
+    for slot in range(RESP):
+        operands, parts = ahead
+        if slot + 1 < RESP:
+            ahead = load(slot + 1)
+        emit(slot, operands, *parts)
     own_out[...] = acc[0]
     far_out[...] = acc[1].astype(jnp.bfloat16)
 
@@ -118,6 +144,7 @@
         scratch_shapes=[
             pltpu.VMEM((2, PROMPT, KV), jnp.bfloat16),
             pltpu.VMEM((2, PROMPT, KV), jnp.float32),
+            pltpu.VMEM((WINDOW, WINDOW), jnp.float32),
         ],
         cost_estimate=pl.CostEstimate(flops=10**9, transcendentals=720896, bytes_accessed=5 * 2**20),
         compiler_params=LARGE,
@@ -174,7 +201,6 @@
         in_specs=[rows, rows],
         out_specs=pl.BlockSpec((KV_HEADS, PROMPT, KV), lambda i: (0, 0, 0)),
         cost_estimate=pl.CostEstimate(flops=0, transcendentals=0, bytes_accessed=2**19),
-        compiler_params=SMALL,
         name="lay_out",
     )(keys, values)
 

time: 141 us -> 139 us (0.986)
  local copies, waits for them, and re-layouts: 7.37 us -> 4.26 us
    unnamed x19 -> x17, local copies, waits for them, and re-layouts: 3.24 us -> 1.35 us
  transfers between devices with their start and end apart: 4 -> 4, of which waited for: 3 -> 3; matrix products, arithmetic and copies ran while one was open for 5% -> 4% of each run, Pallas kernels for 2% -> 2%
where the time goes in v4:
time: 139 us; the launch traced here: 138 us
  blocking collectives  82.7 us (59%)
  starting transfers between devices  24.4 us (18%)
  waiting for transfers between devices  15.2 us (11%)
  Pallas kernels  9.79 us (7%)
  local copies, waits for them, and re-layouts  4.26 us (3%)
    all_gather x2, blocking collectives, exchange(): wanted = pick(partner, lax.all_gather(block, ('z', 'core')))  57 us
    all_gather x2, blocking collectives, exchange(): return lax.all_gather(wanted, 'x', axis=0, tiled=True)  25.7 us
    all_to_all x4, starting transfers between devices, swap(): lax.all_to_all(array, 'head', split_axis=0, concat_axis=0, tiled=True)  24.4 us
    all_to_all x4, waiting for transfers between devices, swap(): lax.all_to_all(array, 'head', split_axis=0, concat_axis=0, tiled=True)  15.2 us
    pallas_call x1, Pallas kernels, attention(): pl.pallas_call(attention_kernel, out_shape=(jax.ShapeDtypeStruct((ROWS, Q...  4.67 us
  transfers between devices with their start and end apart: 4, of which 3 were waited for; matrix products, arithmetic and copies ran while one was open for 4% of the time, Pallas kernels for 2%

profile of v4, /device:TPU:2, one launch (start us, length us, event | category | flops | bytes accessed | tf_op | source)
XLA Modules:
  0.0 138.5 jit_solution(4538209633587915)
XLA Ops:
  0.6 0.0 copy-start.5
  0.6 0.0 copy-start.6
  0.7 0.0 copy-start.7
  0.7 1.8 %lay_out.1 = bf16[8,48,256]{2,1,0:T(8,128)(2,1)} custom-call(bf16[128,1024]{1,0:T(8,128)(2,1)} %keys.1, bf16[128,1024]{1,0:T(8,128)(2,1)} %values.1), custom_call_target="tpu_custom_call" | custom-call | bytes 524288 | tf_op jit(solution)/shard_map/lay_out/pallas_call | solution.py:197
  2.4 7.1 %all-to-all-start.1 = ((bf16[8,48,256]{2,1,0:T(8,128)(2,1)}), bf16[8,48,256]{2,1,0:T(8,128)(2,1)S(1)}, u32[]{:S(2)}, u32[]{:S(2)}) async-start(bf16[8,48,256]{2,1,0:T(8,128)(2,1)} %lay_out.1), calls=%async_computation.1 | async-start | bytes 393216 | tf_op jit(solution)/shard_map/all_to_all | solution.py:264
  9.5 0.0 copy-done.5
  9.5 0.1 copy.30
  9.6 0.0 copy-done.6
  9.6 0.0 copy-done.7
  9.6 0.1 bitcast_bitcast_fusion.1
  9.8 1.3 pad_maximum_fusion
  11.1 0.0 copy-start
  11.1 8.9 %all-to-all-done.1 = bf16[8,48,256]{2,1,0:T(8,128)(2,1)S(1)} async-done(((bf16[8,48,256]{2,1,0:T(8,128)(2,1)}), bf16[8,48,256]{2,1,0:T(8,128)(2,1)S(1)}, u32[]{:S(2)}, u32[]{:S(2)}) %all-to-all-start.1) | async-done | bytes 196640 | tf_op jit(solution)/shard_map/all_to_all | solution.py:264
  20.0 3.6 %all-to-all-start = ((bf16[8,128,768]{2,1,0:T(8,128)(2,1)}), bf16[8,128,768]{2,1,0:T(8,128)(2,1)S(1)}, u32[]{:S(2)}, u32[]{:S(2)}) async-start(bf16[8,128,768]{2,1,0:T(8,128)(2,1)} %pad_maximum_fusion), calls=%async_computation | async-start | bytes 3145728 | tf_op jit(solution)/shard_map/all_to_all | solution.py:264
  23.6 0.0 copy-start.1
  23.6 0.0 copy-start.2
  23.6 0.0 copy-start.3
  23.6 0.0 copy-start.4
  23.6 34.8 %all_gather.15.blocks = bf16[24,48,256]{2,1,0:T(8,128)(2,1)S(1)} all-gather(bf16[1,48,256]{2,1,0:T(8,128)(2,1)S(1)} %slice.8), channel_id=1, replica_groups=mesh['x'=4,'z'=12,'core'=2,'head'=8] {'z','core'}, dimensions={0}, use_global_device_ids=true | all-gather | bytes 614400 | tf_op jit(solution)/shard_map/all_gather | solution.py:179
  58.5 0.0 copy-done
  58.5 0.6 pick.2
  59.1 13.0 %all_gather.16.far_in = bf16[16,48,256]{2,1,0:T(8,128)(2,1)S(1)} all-gather(bf16[4,48,256]{2,1,0:T(8,128)(2,1)S(1)} %pick.2), channel_id=1, replica_groups=mesh['x'=4,'z'=12,'core'=2,'head'=8] {'x'}, dimensions={0}, use_global_device_ids=true | all-gather | bytes 491520 | tf_op jit(solution)/shard_map/all_gather | solution.py:180
  72.1 0.0 all-to-all-done
  72.1 0.0 copy-done.1
  72.1 0.0 copy-done.2
  72.1 0.0 copy-done.3
  72.1 0.0 copy-done.4
  72.1 4.7 %attention.1 = (bf16[1024,768]{1,0:T(8,128)(2,1)}, bf16[48,256]{1,0:T(8,128)(2,1)S(1)}, f32[48,256]{1,0:T(8,128)S(1)}) custom-call(s32[96]{0:T(128)S(1)} %copy-done, s32[1,8]{1,0:T(1,128)S(1)} %copy-done.2, s32[1,8]{1,0:T(1,128)S(1)} %copy-done.3, f32[1,8]{1,0:T(1,128)S(1)} %copy-done.4, bf16[1024,768]{1,0:T(8,128)(2,1)S(1)} %bitcast.28, ...), custom_call_target="tpu_custom_call" | custom-call | flops 1000000000 | bytes 5242880 | tf_op jit(solution)/shard_map/attention/pallas_call | solution.py:135
  76.8 7.1 %all-to-all-start.2 = ((bf16[8,128,768]{2,1,0:T(8,128)(2,1)}), bf16[8,128,768]{2,1,0:T(8,128)(2,1)S(1)}, u32[]{:S(2)}, u32[]{:S(2)}) async-start(bf16[8,128,768]{2,1,0:T(8,128)(2,1)} %bitcast.5), calls=%async_computation.2 | async-start | bytes 3145728 | tf_op jit(solution)/shard_map/all_to_all | solution.py:264
  83.9 22.1 %all-gather = bf16[1152,256]{1,0:T(8,128)(2,1)S(1)} all-gather(bf16[48,256]{1,0:T(8,128)(2,1)S(1)} %get-tuple-element.11), channel_id=2, replica_groups=mesh['x'=4,'z'=12,'core'=2,'head'=8] {'z','core'}, dimensions={0}, use_global_device_ids=true | all-gather | bytes 614400 | tf_op jit(solution)/shard_map/all_gather | solution.py:179
  106.0 0.6 pick.3
  106.5 12.8 %all_gather.19.back = bf16[16,48,256]{2,1,0:T(8,128)(2,1)S(1)} all-gather(bf16[4,48,256]{2,1,0:T(8,128)(2,1)S(1)} %pick.3), channel_id=1, replica_groups=mesh['x'=4,'z'=12,'core'=2,'head'=8] {'x'}, dimensions={0}, use_global_device_ids=true | all-gather | bytes 491520 | tf_op jit(solution)/shard_map/all_gather | solution.py:180
  119.3 1.3 finish.1
  120.6 0.5 all-to-all-done.2.main
  121.1 6.7 %all-to-all-start.3 = ((bf16[8,48,256]{2,1,0:T(8,128)(2,1)}), bf16[8,48,256]{2,1,0:T(8,128)(2,1)S(1)}, u32[]{:S(2)}, u32[]{:S(2)}) async-start(bf16[8,48,256]{2,1,0:T(8,128)(2,1)} %finish.1), calls=%async_computation.3 | async-start | bytes 393216 | tf_op jit(solution)/shard_map/all_to_all | solution.py:264
  127.7 1.1 slice_bitcast_fusion
  128.8 1.6 %copy.22 = bf16[128,8,512]{0,2,1:T(8,128)(2,1)S(1)} copy(bf16[128,8,512]{2,0,1:T(8,128)(2,1)} %slice_bitcast_fusion) | data formatting | bytes 2097152 | tf_op jit(solution)/shard_map/transpose | solution.py:276
  130.4 1.3 copy.23
  131.7 5.8 %all-to-all-done.3.first = bf16[8,48,256]{2,1,0:T(8,128)(2,1)S(1)} async-done(((bf16[8,48,256]{2,1,0:T(8,128)(2,1)}), bf16[8,48,256]{2,1,0:T(8,128)(2,1)S(1)}, u32[]{:S(2)}, u32[]{:S(2)}) %all-to-all-start.3) | async-done | bytes 196640 | tf_op jit(solution)/shard_map/all_to_all | solution.py:264
  137.5 0.9 by_token.1
  (1 shorter events, 0.0 us)
Async XLA Ops:
  0.6 8.9 %copy-start.5 = (bf16[128,4096]{1,0:T(8,128)(2,1)S(1)}, bf16[128,4096]{1,0:T(8,128)(2,1)}, u32[]{:S(2)}) copy-start(bf16[128,4096]{1,0:T(8,128)(2,1)} %param.8) | copy-start | bytes 3145732
  0.6 9.0 %copy-start.6 = (bf16[128,1024]{1,0:T(8,128)(2,1)S(1)}, bf16[128,1024]{1,0:T(8,128)(2,1)}, u32[]{:S(2)}) copy-start(bf16[128,1024]{1,0:T(8,128)(2,1)} %keys.1) | copy-start | bytes 786436
  0.7 9.0 %copy-start.7 = (bf16[128,1024]{1,0:T(8,128)(2,1)S(1)}, bf16[128,1024]{1,0:T(8,128)(2,1)}, u32[]{:S(2)}) copy-start(bf16[128,1024]{1,0:T(8,128)(2,1)} %values.1) | copy-start | bytes 786436
  2.4 17.6 %all-to-all-start.1 = ((bf16[8,48,256]{2,1,0:T(8,128)(2,1)}), bf16[8,48,256]{2,1,0:T(8,128)(2,1)S(1)}, u32[]{:S(2)}, u32[]{:S(2)}) async-start(bf16[8,48,256]{2,1,0:T(8,128)(2,1)} %lay_out.1), calls=%async_computation.1 | async-start | bytes 393216 | tf_op jit(solution)/shard_map/all_to_all | solution.py:264
  11.1 47.4 %copy-start = (s32[96]{0:T(128)S(1)}, s32[96]{0:T(128)}, u32[]{:S(2)}) copy-start(s32[96]{0:T(128)} %partner.7) | copy-start | bytes 1156
  20.0 52.1 %all-to-all-start = ((bf16[8,128,768]{2,1,0:T(8,128)(2,1)}), bf16[8,128,768]{2,1,0:T(8,128)(2,1)S(1)}, u32[]{:S(2)}, u32[]{:S(2)}) async-start(bf16[8,128,768]{2,1,0:T(8,128)(2,1)} %pad_maximum_fusion), calls=%async_computation | async-start | bytes 3145728 | tf_op jit(solution)/shard_map/all_to_all | solution.py:264
  23.6 48.5 %copy-start.1 = (bf16[1024,512]{1,0:T(8,128)(2,1)S(1)}, bf16[1024,512]{1,0:T(8,128)(2,1)}, u32[]{:S(2)}) copy-start(bf16[1024,512]{1,0:T(8,128)(2,1)} %cot_ref.1) | copy-start | bytes 3145732
  23.6 48.5 %copy-start.2 = (s32[1,8]{1,0:T(1,128)S(1)}, s32[1,8]{1,0:T(1,128)}, u32[]{:S(2)}) copy-start(s32[1,8]{1,0:T(1,128)} %lengths.1) | copy-start | bytes 100
  23.6 48.5 %copy-start.3 = (s32[1,8]{1,0:T(1,128)S(1)}, s32[1,8]{1,0:T(1,128)}, u32[]{:S(2)}) copy-start(s32[1,8]{1,0:T(1,128)} %guests.1) | copy-start | bytes 100
  23.6 48.5 %copy-start.4 = (f32[1,8]{1,0:T(1,128)S(1)}, f32[1,8]{1,0:T(1,128)}, u32[]{:S(2)}) copy-start(f32[1,8]{1,0:T(1,128)} %adv.1) | copy-start | bytes 100
  76.8 44.3 %all-to-all-start.2 = ((bf16[8,128,768]{2,1,0:T(8,128)(2,1)}), bf16[8,128,768]{2,1,0:T(8,128)(2,1)S(1)}, u32[]{:S(2)}, u32[]{:S(2)}) async-start(bf16[8,128,768]{2,1,0:T(8,128)(2,1)} %bitcast.5), calls=%async_computation.2 | async-start | bytes 3145728 | tf_op jit(solution)/shard_map/all_to_all | solution.py:264
  121.1 16.4 %all-to-all-start.3 = ((bf16[8,48,256]{2,1,0:T(8,128)(2,1)}), bf16[8,48,256]{2,1,0:T(8,128)(2,1)S(1)}, u32[]{:S(2)}, u32[]{:S(2)}) async-start(bf16[8,48,256]{2,1,0:T(8,128)(2,1)} %finish.1), calls=%async_computation.3 | async-start | bytes 393216 | tf_op jit(solution)/shard_map/all_to_all | solution.py:264

commit v5 on v4

--- a/solution.py
+++ b/solution.py
@@ -15,6 +15,9 @@
 WINDOW = 128
 Q = GROUP * HEAD_DIM
 KV = 2 * HEAD_DIM
+BLOCK = ROWS // KV_HEADS
+REST = BLOCK - PROMPT
+PACKED = REST + 2 * BLOCK
 TREES = ("x", "z", "core")
 PLANE = ("x", "core")
 X, Z, CORE = 4, 12, 2
@@ -50,20 +53,55 @@
     )
 
 
-def unstack_heads(block, rows):
-    return jnp.concatenate([block[j * rows : (j + 1) * rows] for j in range(GROUP)], axis=1)
+def segments(start, rows):
+    found, at = [], start
+    while at < start + rows:
+        block, first = divmod(at, BLOCK)
+        last = min(PROMPT if first < PROMPT else BLOCK, first + start + rows - at)
+        found.append((block, first, last, at - start))
+        at += last - first
+    return found
+
+
+def q_index(block, first, last, head):
+    shift = REST + head // 2 * BLOCK
+    lanes = slice(head % 2 * HEAD_DIM, (head % 2 + 1) * HEAD_DIM)
+    return block, slice(shift + first, shift + last), lanes
+
+
+def kv_index(packed, low, block, first, last):
+    if first < PROMPT:
+        return low, (block, slice(first, last))
+    return packed, (block, slice(first - PROMPT, last - PROMPT))
 
 
 def attention_kernel(
-    partner, lengths, guests, adv, qkv, cot_ref, far_in, grads, far_out, own_out, pre, acc, later
+    partner, lengths, guests, adv, packed, low, cot_ref, far_in, grads, grads_low, far_out, own_out, pre, acc, later
 ):
     iota = lax.broadcasted_iota
-    pre[0] = qkv[:PROMPT, Q:]
+    pre[0] = low[0]
     pre[1] = far_in[partner_entry(partner)]
     acc[1] = jnp.zeros((PROMPT, KV), jnp.float32)
     causal = iota(jnp.int32, later.shape, 0) <= iota(jnp.int32, later.shape, 1)
     later[...] = jnp.where(causal, 0.0, -jnp.inf)
 
+    def q_of(start, rows):
+        return jnp.concatenate(
+            [
+                packed[q_index(block, first, last, head)]
+                for head in range(GROUP)
+                for block, first, last, _ in segments(start, rows)
+            ],
+            axis=0,
+        )
+
+    def kv_of(start, rows):
+        parts = []
+        for block, first, last, _ in segments(start, rows):
+            ref, index = kv_index(packed, low, block, first, last)
+            parts.append(ref[index])
+        return parts
+
     def window(slot):
         first = PROMPT + RESP_LEN * slot
         start = first // 8 * 8
@@ -72,9 +110,9 @@
     def load(slot):
         rows, skip = window(slot)
         guest = guests[0, slot]
-        q_rows = stack_heads(qkv[rows, :Q])
-        keys = jnp.concatenate([pre[guest, :, :HEAD_DIM], qkv[rows, Q : Q + HEAD_DIM]], axis=0)
-        vals = jnp.concatenate([pre[guest, :, HEAD_DIM:], qkv[rows, Q + HEAD_DIM :]], axis=0)
+        q_rows = q_of(rows.start, WINDOW)
+        kv = jnp.concatenate([pre[guest]] + kv_of(rows.start, WINDOW), axis=0)
+        keys, vals = kv[:, :HEAD_DIM], kv[:, HEAD_DIM:]
         token = iota(jnp.int32, (WINDOW, HEAD_DIM), 0) - skip
         weight = jnp.where((token >= 0) & (token < lengths[0, slot]), adv[0, slot], 0.0)
         cot = jnp.concatenate(
@@ -96,14 +134,23 @@
         scores = jnp.concatenate([scores[:PROMPT], scores[PROMPT:] + bias], axis=0)
         grad_q, grad_kv = backward(scores, grad_probs, *operands)
         acc[guests[0, slot]] += grad_kv[:PROMPT]
-        new = jnp.concatenate([unstack_heads(grad_q, WINDOW), grad_kv[PROMPT:]], axis=1)
+        for block, first, last, at in segments(rows.start, WINDOW):
+            for head in range(GROUP):
+                new = grad_q[head * WINDOW + at : head * WINDOW + at + last - first]
+                store(grads, q_index(block, first, last, head), new, skip if at == 0 else 0)
+            ref, index = kv_index(grads, grads_low, block, first, last)
+            new = grad_kv[PROMPT + at : PROMPT + at + last - first]
+            store(ref, index, new, skip if at == 0 else 0)
+
+    def store(ref, index, new, skip):
         if skip:
-            old = grads[rows.start : rows.start + 8, :].astype(jnp.float32)
+            block, rows, *lanes = index
+            old = ref[(block, slice(rows.start, rows.start + 8), *lanes)].astype(jnp.float32)
             top = jnp.where(iota(jnp.int32, old.shape, 0) < skip, old, new[:8])
-            new = jnp.concatenate([top, new[8:]], axis=0)
-        grads[rows, :] = new.astype(jnp.bfloat16)
-
-    q_rows = stack_heads(qkv[:PROMPT, :Q])
+            new = jnp.concatenate([top, new[8:]], axis=0) if new.shape[0] > 8 else top
+        ref[index] = new.astype(jnp.bfloat16)
+
+    q_rows = q_of(0, PROMPT)
     cot = stack_heads(cot_ref[:PROMPT, :])
     keys = pre[0, :, :HEAD_DIM]
     scores, grad_probs = products(q_rows, keys, pre[0, :, HEAD_DIM:], cot)
@@ -112,8 +159,9 @@
         query = jnp.where(query >= PROMPT, query - PROMPT, query)
     scores = jnp.where(iota(jnp.int32, scores.shape, 0) <= query, scores, -jnp.inf)
     grad_q, acc[0] = backward(scores, grad_probs, q_rows, keys, cot)
-    grads[:PROMPT, :Q] = unstack_heads(grad_q, PROMPT).astype(jnp.bfloat16)
-    grads[:PROMPT, Q:] = jnp.zeros((PROMPT, KV), jnp.bfloat16)
+    for head in range(GROUP):
+        new = grad_q[head * PROMPT : (head + 1) * PROMPT]
+        store(grads, q_index(0, 0, PROMPT, head), new, 0)
 
     ahead = load(0)
     for slot in range(RESP):
@@ -122,6 +170,7 @@
             ahead = load(slot + 1)
         emit(slot, operands, *parts)
     own_out[...] = acc[0]
+    grads_low[0] = acc[0].astype(jnp.bfloat16)
     far_out[...] = acc[1].astype(jnp.bfloat16)
 
 
@@ -131,16 +180,17 @@
 LARGE = pltpu.CompilerParams(vmem_limit_bytes=24 * 2**20)
 
 
-def attention(partner, lengths, guests, adv, qkv, cot, far):
+def attention(partner, lengths, guests, adv, packed, low, cot, far):
     return pl.pallas_call(
         attention_kernel,
         out_shape=(
-            jax.ShapeDtypeStruct((ROWS, Q + KV), jnp.bfloat16),
+            jax.ShapeDtypeStruct(packed.shape, jnp.bfloat16),
+            jax.ShapeDtypeStruct(low.shape, jnp.bfloat16),
             jax.ShapeDtypeStruct((PROMPT, KV), jnp.bfloat16),
             jax.ShapeDtypeStruct((PROMPT, KV), jnp.float32),
         ),
-        in_specs=[SMEM] * 4 + [VMEM] * 3,
-        out_specs=(VMEM, VMEM, VMEM),
+        in_specs=[SMEM] * 4 + [VMEM] * 4,
+        out_specs=(VMEM,) * 4,
         scratch_shapes=[
             pltpu.VMEM((2, PROMPT, KV), jnp.bfloat16),
             pltpu.VMEM((2, PROMPT, KV), jnp.float32),
@@ -149,7 +199,7 @@
         cost_estimate=pl.CostEstimate(flops=10**9, transcendentals=720896, bytes_accessed=5 * 2**20),
         compiler_params=LARGE,
         name="attention",
-    )(partner, lengths, guests, adv, qkv, cot, far)
+    )(partner, lengths, guests, adv, packed, low, cot, far)
 
 
 def place():
@@ -205,76 +255,106 @@
     )(keys, values)
 
 
-def by_token_kernel(main, first, grad_k, grad_v):
-    owner = lax.axis_index("head") == 0
+def pack_kernel(queries, keys, values, out):
+    for i in range(KV_HEADS):
+        lanes = slice(i * HEAD_DIM, (i + 1) * HEAD_DIM)
+        out[i, :REST, :HEAD_DIM] = keys[PROMPT:, lanes]
+        out[i, :REST, HEAD_DIM:] = values[PROMPT:, lanes]
+        out[i, REST : REST + BLOCK] = queries[:, i * Q : i * Q + KV]
+        out[i, REST + BLOCK :] = queries[:, i * Q + KV : (i + 1) * Q]
+
+
+def pack(queries, keys, values):
+    return pl.pallas_call(
+        pack_kernel,
+        out_shape=jax.ShapeDtypeStruct((KV_HEADS, PACKED, KV), jnp.bfloat16),
+        in_specs=[VMEM] * 3,
+        out_specs=VMEM,
+        cost_estimate=pl.CostEstimate(flops=0, transcendentals=0, bytes_accessed=3 * 2**20),
+        compiler_params=SMALL,
+        name="pack",
+    )(queries, keys, values)
+
+
+def q_by_token_kernel(grads, out):
+    for i in range(KV_HEADS):
+        out[:, i * Q : i * Q + KV] = grads[i, REST : REST + BLOCK]
+        out[:, i * Q + KV : (i + 1) * Q] = grads[i, REST + BLOCK :]
+
+
+def q_by_token(grads):
+    return pl.pallas_call(
+        q_by_token_kernel,
+        out_shape=jax.ShapeDtypeStruct((BLOCK, KV_HEADS * Q), jnp.bfloat16),
+        in_specs=[VMEM],
+        out_specs=VMEM,
+        cost_estimate=pl.CostEstimate(flops=0, transcendentals=0, bytes_accessed=2 * 2**20),
+        compiler_params=SMALL,
+        name="q_by_token",
+    )(grads)
+
+
+def kv_by_token_kernel(rest, low, grad_k, grad_v):
     for i in range(KV_HEADS):
         lanes = slice(i * HEAD_DIM, (i + 1) * HEAD_DIM)
         for ref, start in ((grad_k, 0), (grad_v, HEAD_DIM)):
             part = slice(start, start + HEAD_DIM)
-            old = main[i, :PROMPT, part].astype(jnp.float32)
-            top = jnp.where(owner, first[i, :, part].astype(jnp.float32), old)
-            ref[:PROMPT, lanes] = top.astype(ref.dtype)
-            ref[PROMPT:, lanes] = main[i, PROMPT:, part]
-
-
-def by_token(grads, first):
-    rows = grads.shape[1]
-    out = jax.ShapeDtypeStruct((rows, KV_HEADS * HEAD_DIM), jnp.bfloat16)
+            ref[:PROMPT, lanes] = low[i, :, part]
+            ref[PROMPT:, lanes] = rest[i, :, part]
+
+
+def kv_by_token(grads, low):
+    out = jax.ShapeDtypeStruct((BLOCK, KV_HEADS * HEAD_DIM), jnp.bfloat16)
     whole = pl.BlockSpec(out.shape, lambda i: (0, 0))
     return pl.pallas_call(
-        by_token_kernel,
+        kv_by_token_kernel,
         grid=(1,),
         out_shape=(out, out),
         in_specs=[
-            pl.BlockSpec((KV_HEADS, rows, KV), lambda i: (0, 0, Q // KV)),
+            pl.BlockSpec((KV_HEADS, REST, KV), lambda i: (0, 0, 0)),
             pl.BlockSpec((KV_HEADS, PROMPT, KV), lambda i: (0, 0, 0)),
         ],
         out_specs=(whole, whole),
         cost_estimate=pl.CostEstimate(flops=0, transcendentals=0, bytes_accessed=2**20),
         compiler_params=SMALL,
-        name="by_token",
-    )(grads, first)
-
-
-def finish_kernel(partner, own, back, out):
-    block = own[...] + back[partner_entry(partner)].astype(jnp.float32)
-    for i in range(KV_HEADS):
-        out[i] = block.astype(out.dtype)
-
-
-def finish(partner, own, back):
+        name="kv_by_token",
+    )(grads, low)
+
+
+def finish_kernel(partner, own, back, low, out):
+    total = own[...] + back[partner_entry(partner)].astype(jnp.float32)
+    out[0] = total.astype(out.dtype)
+    for i in range(1, KV_HEADS):
+        out[i] = low[i]
+
+
+def finish(partner, own, back, low):
     return pl.pallas_call(
         finish_kernel,
-        out_shape=jax.ShapeDtypeStruct((KV_HEADS,) + own.shape, jnp.bfloat16),
-        in_specs=[SMEM, VMEM, VMEM],
+        out_shape=jax.ShapeDtypeStruct(low.shape, jnp.bfloat16),
+        in_specs=[SMEM, VMEM, VMEM, VMEM],
         out_specs=VMEM,
         cost_estimate=pl.CostEstimate(flops=0, transcendentals=0, bytes_accessed=2**18),
         compiler_params=SMALL,
         name="finish",
-    )(partner, own, back)
+    )(partner, own, back, low)
 
 
 def local(queries, keys, values, upstream, lengths, guests, advantage, partner):
-    rows = queries.shape[0]
-
-    def by_head(array):
-        return array.reshape(array.shape[0], KV_HEADS, -1).transpose(1, 0, 2)
-
     def swap(array):
         return lax.all_to_all(array, "head", split_axis=0, concat_axis=0, tiled=True)
 
-    prompt = swap(lay_out(keys, values))
-    qkv = swap(jnp.concatenate([by_head(queries), by_head(keys), by_head(values)], axis=2))
-    far = exchange(prompt[0], partner)
-    grads, far_grad, own = attention(
-        partner, lengths, guests, advantage, qkv.reshape(ROWS, -1), upstream, far
+    low = swap(lay_out(keys, values))
+    packed = swap(pack(queries, keys, values))
+    far = exchange(low[0], partner)
+    grads, grads_low, far_grad, own = attention(
+        partner, lengths, guests, advantage, packed, low, upstream, far
     )
-    grads = swap(grads.reshape(KV_HEADS, rows, -1))
-    first = finish(partner, own, exchange(far_grad, partner))
-    first, grads = lax.optimization_barrier((first, grads))
-    first = swap(first)
-    grad_q = grads[:, :, :Q].transpose(1, 0, 2).reshape(rows, -1)
-    return (grad_q,) + tuple(by_token(grads, first))
+    grads = swap(grads)
+    grads_low = finish(partner, own, exchange(far_grad, partner), grads_low)
+    grads_low, grads = lax.optimization_barrier((grads_low, grads))
+    grads_low = swap(grads_low)
+    return (q_by_token(grads),) + tuple(kv_by_token(grads, grads_low))
 
 
 def solution(mesh):

time: 139 us -> 139 us (level)
  local copies, waits for them, and re-layouts: 4.26 us -> 1.93 us
  Pallas kernels: 9.79 us -> 12 us
    transpose x3 -> x0, local copies, waits for them, and re-layouts: 2.82 us -> none  [the longest x2 2.7 us: local(): grad_q = grads[:, :, :Q].transpose(1, 0, 2).reshape(rows, -1)]
    pallas_call x3 -> x5, Pallas kernels: 6.88 us -> 9.07 us  [the longest x1 4.58 us: attention(): pl.pallas_call(attention_kernel, out_shape=(jax.ShapeDtypeStruct(packed.s...]
  transfers between devices with their start and end apart: 4 -> 4, of which waited for: 3 -> 2; matrix products, arithmetic and copies ran while one was open for 4% -> 0% of each run, Pallas kernels for 2% -> 3%
where the time goes in v5:
time: 139 us
  blocking collectives  82.6 us (59%)
  starting transfers between devices  25.3 us (18%)
  waiting for transfers between devices  16.1 us (12%)
  Pallas kernels  12 us (9%)
  local copies, waits for them, and re-layouts  1.93 us (1%)
    all_gather x2, blocking collectives, exchange(): wanted = pick(partner, lax.all_gather(block, ('z', 'core')))  57 us
    all_gather x2, blocking collectives, exchange(): return lax.all_gather(wanted, 'x', axis=0, tiled=True)  25.7 us
    all_to_all x4, starting transfers between devices, swap(): lax.all_to_all(array, 'head', split_axis=0, concat_axis=0, tiled=True)  25.3 us
    all_to_all x4, waiting for transfers between devices, swap(): lax.all_to_all(array, 'head', split_axis=0, concat_axis=0, tiled=True)  16.1 us
    pallas_call x1, Pallas kernels, attention(): pl.pallas_call(attention_kernel, out_shape=(jax.ShapeDtypeStruct(packed.s...  4.58 us
  transfers between devices with their start and end apart: 4, of which 2 were waited for; matrix products, arithmetic and copies ran while one was open for 0% of the time, Pallas kernels for 3%

profile of v5, /device:TPU:2, one launch (start us, length us, event | category | flops | bytes accessed | tf_op | source)
XLA Modules:
  0.0 138.6 jit_solution(15026437136888593473)
XLA Ops:
  0.6 0.0 copy-start
  0.6 1.7 %lay_out.1 = bf16[8,48,256]{2,1,0:T(8,128)(2,1)} custom-call(bf16[128,1024]{1,0:T(8,128)(2,1)} %keys.3, bf16[128,1024]{1,0:T(8,128)(2,1)} %values.3), custom_call_target="tpu_custom_call" | custom-call | bytes 524288 | tf_op jit(solution)/shard_map/lay_out/pallas_call | solution.py:247
  2.4 7.1 %all-to-all-start.1 = ((bf16[8,48,256]{2,1,0:T(8,128)(2,1)}), bf16[8,48,256]{2,1,0:T(8,128)(2,1)S(1)}, u32[]{:S(2)}, u32[]{:S(2)}) async-start(bf16[8,48,256]{2,1,0:T(8,128)(2,1)} %lay_out.1), calls=%async_computation.1 | async-start | bytes 393216 | tf_op jit(solution)/shard_map/all_to_all | solution.py:345
  9.5 0.0 copy-done
  9.5 0.0 copy-start.1
  9.5 0.9 copy-done.1
  10.4 0.0 copy-start.2
  10.4 0.9 copy-done.2
  11.4 1.2 pack.1
  12.6 0.0 copy-start.3
  12.6 7.3 %all-to-all-done.1.low = bf16[8,48,256]{2,1,0:T(8,128)(2,1)S(1)} async-done(((bf16[8,48,256]{2,1,0:T(8,128)(2,1)}), bf16[8,48,256]{2,1,0:T(8,128)(2,1)S(1)}, u32[]{:S(2)}, u32[]{:S(2)}) %all-to-all-start.1) | async-done | bytes 196640 | tf_op jit(solution)/shard_map/all_to_all | solution.py:345
  20.0 3.6 %all-to-all-start = ((bf16[8,336,256]{2,1,0:T(8,128)(2,1)}), bf16[8,336,256]{2,1,0:T(8,128)(2,1)S(1)}, u32[]{:S(2)}, u32[]{:S(2)}) async-start(bf16[8,336,256]{2,1,0:T(8,128)(2,1)} %pack.1), calls=%async_computation | async-start | bytes 2752512 | tf_op jit(solution)/shard_map/all_to_all | solution.py:345
  23.5 0.0 copy-start.4
  23.5 0.0 copy-start.5
  23.6 0.0 copy-start.6
  23.6 0.0 copy-start.7
  23.6 34.8 %all_gather.15.blocks = bf16[24,48,256]{2,1,0:T(8,128)(2,1)S(1)} all-gather(bf16[1,48,256]{2,1,0:T(8,128)(2,1)S(1)} %slice.4), channel_id=1, replica_groups=mesh['x'=4,'z'=12,'core'=2,'head'=8] {'z','core'}, dimensions={0}, use_global_device_ids=true | all-gather | bytes 614400 | tf_op jit(solution)/shard_map/all_gather | solution.py:229
  58.4 0.0 copy-done.3
  58.4 0.6 pick.2
  59.0 13.0 %all_gather.16.far_in = bf16[16,48,256]{2,1,0:T(8,128)(2,1)S(1)} all-gather(bf16[4,48,256]{2,1,0:T(8,128)(2,1)S(1)} %pick.2), channel_id=1, replica_groups=mesh['x'=4,'z'=12,'core'=2,'head'=8] {'x'}, dimensions={0}, use_global_device_ids=true | all-gather | bytes 491520 | tf_op jit(solution)/shard_map/all_gather | solution.py:230
  72.0 0.0 all-to-all-done.packed
  72.0 0.0 copy-done.4
  72.0 0.0 copy-done.5
  72.0 0.0 copy-done.6
  72.0 0.0 copy-done.7
  72.0 4.6 %attention.1 = (bf16[8,336,256]{2,1,0:T(8,128)(2,1)}, bf16[8,48,256]{2,1,0:T(8,128)(2,1)S(1)}, bf16[48,256]{1,0:T(8,128)(2,1)S(1)}, f32[48,256]{1,0:T(8,128)S(1)}) custom-call(s32[96]{0:T(128)S(1)} %copy-done.3, s32[1,8]{1,0:T(1,128)S(1)} %copy-done.5, s32[1,8]{1,0:T(1,128)S(1)} %copy-done.6, f32[1,8]{1,0:T(1,128)S(1)} %copy-done.7, ...), custom_call_target="tpu_custom_call" | custom-call | flops 1000000000 | bytes 5242880 | tf_op jit(solution)/shard_map/attention/pallas_call | solution.py:184
  76.6 7.1 %all-to-all-start.2 = ((bf16[8,336,256]{2,1,0:T(8,128)(2,1)}), bf16[8,336,256]{2,1,0:T(8,128)(2,1)S(1)}, u32[]{:S(2)}, u32[]{:S(2)}) async-start(bf16[8,336,256]{2,1,0:T(8,128)(2,1)} %get-tuple-element.14), calls=%async_computation.2 | async-start | bytes 2752512 | tf_op jit(solution)/shard_map/all_to_all | solution.py:345
  83.7 22.1 %all-gather = bf16[1152,256]{1,0:T(8,128)(2,1)S(1)} all-gather(bf16[48,256]{1,0:T(8,128)(2,1)S(1)} %get-tuple-element.12), channel_id=2, replica_groups=mesh['x'=4,'z'=12,'core'=2,'head'=8] {'z','core'}, dimensions={0}, use_global_device_ids=true | all-gather | bytes 614400 | tf_op jit(solution)/shard_map/all_gather | solution.py:229
  105.8 0.6 pick.3
  106.4 12.7 %all_gather.19.back = bf16[16,48,256]{2,1,0:T(8,128)(2,1)S(1)} all-gather(bf16[4,48,256]{2,1,0:T(8,128)(2,1)S(1)} %pick.3), channel_id=1, replica_groups=mesh['x'=4,'z'=12,'core'=2,'head'=8] {'x'}, dimensions={0}, use_global_device_ids=true | all-gather | bytes 491520 | tf_op jit(solution)/shard_map/all_gather | solution.py:230
  119.1 1.3 finish.1
  120.3 0.0 all-to-all-done.2.grads.rest
  120.3 7.5 %all-to-all-start.3 = ((bf16[8,48,256]{2,1,0:T(8,128)(2,1)}), bf16[8,48,256]{2,1,0:T(8,128)(2,1)S(1)}, u32[]{:S(2)}, u32[]{:S(2)}) async-start(bf16[8,48,256]{2,1,0:T(8,128)(2,1)} %finish.1), calls=%async_computation.3 | async-start | bytes 393216 | tf_op jit(solution)/shard_map/all_to_all | solution.py:345
  127.8 1.1 q_by_token.1
  128.9 8.7 %all-to-all-done.3.low = bf16[8,48,256]{2,1,0:T(8,128)(2,1)S(1)} async-done(((bf16[8,48,256]{2,1,0:T(8,128)(2,1)}), bf16[8,48,256]{2,1,0:T(8,128)(2,1)S(1)}, u32[]{:S(2)}, u32[]{:S(2)}) %all-to-all-start.3) | async-done | bytes 196640 | tf_op jit(solution)/shard_map/all_to_all | solution.py:345
  137.6 1.0 kv_by_token.1
  (1 shorter events, 0.0 us)
Async XLA Ops:
  0.6 8.9 %copy-start = (bf16[128,4096]{1,0:T(8,128)(2,1)S(1)}, bf16[128,4096]{1,0:T(8,128)(2,1)}, u32[]{:S(2)}) copy-start(bf16[128,4096]{1,0:T(8,128)(2,1)} %queries.1) | copy-start | bytes 3145732
  2.4 17.6 %all-to-all-start.1 = ((bf16[8,48,256]{2,1,0:T(8,128)(2,1)}), bf16[8,48,256]{2,1,0:T(8,128)(2,1)S(1)}, u32[]{:S(2)}, u32[]{:S(2)}) async-start(bf16[8,48,256]{2,1,0:T(8,128)(2,1)} %lay_out.1), calls=%async_computation.1 | async-start | bytes 393216 | tf_op jit(solution)/shard_map/all_to_all | solution.py:345
  9.5 1.0 copy-start.1
  10.4 0.9 copy-start.2
  12.6 45.8 %copy-start.3 = (s32[96]{0:T(128)S(1)}, s32[96]{0:T(128)}, u32[]{:S(2)}) copy-start(s32[96]{0:T(128)} %partner.7) | copy-start | bytes 1156
  20.0 52.0 %all-to-all-start = ((bf16[8,336,256]{2,1,0:T(8,128)(2,1)}), bf16[8,336,256]{2,1,0:T(8,128)(2,1)S(1)}, u32[]{:S(2)}, u32[]{:S(2)}) async-start(bf16[8,336,256]{2,1,0:T(8,128)(2,1)} %pack.1), calls=%async_computation | async-start | bytes 2752512 | tf_op jit(solution)/shard_map/all_to_all | solution.py:345
  23.5 48.5 %copy-start.4 = (bf16[1024,512]{1,0:T(8,128)(2,1)S(1)}, bf16[1024,512]{1,0:T(8,128)(2,1)}, u32[]{:S(2)}) copy-start(bf16[1024,512]{1,0:T(8,128)(2,1)} %cot_ref.1) | copy-start | bytes 3145732
  23.5 48.5 %copy-start.5 = (s32[1,8]{1,0:T(1,128)S(1)}, s32[1,8]{1,0:T(1,128)}, u32[]{:S(2)}) copy-start(s32[1,8]{1,0:T(1,128)} %lengths.1) | copy-start | bytes 100
  23.6 48.5 %copy-start.6 = (s32[1,8]{1,0:T(1,128)S(1)}, s32[1,8]{1,0:T(1,128)}, u32[]{:S(2)}) copy-start(s32[1,8]{1,0:T(1,128)} %guests.1) | copy-start | bytes 100
  23.6 48.5 %copy-start.7 = (f32[1,8]{1,0:T(1,128)S(1)}, f32[1,8]{1,0:T(1,128)}, u32[]{:S(2)}) copy-start(f32[1,8]{1,0:T(1,128)} %adv.1) | copy-start | bytes 100
  76.6 43.7 %all-to-all-start.2 = ((bf16[8,336,256]{2,1,0:T(8,128)(2,1)}), bf16[8,336,256]{2,1,0:T(8,128)(2,1)S(1)}, u32[]{:S(2)}, u32[]{:S(2)}) async-start(bf16[8,336,256]{2,1,0:T(8,128)(2,1)} %get-tuple-element.14), calls=%async_computation.2 | async-start | bytes 2752512 | tf_op jit(solution)/shard_map/all_to_all | solution.py:345
  120.3 17.3 %all-to-all-start.3 = ((bf16[8,48,256]{2,1,0:T(8,128)(2,1)}), bf16[8,48,256]{2,1,0:T(8,128)(2,1)S(1)}, u32[]{:S(2)}, u32[]{:S(2)}) async-start(bf16[8,48,256]{2,1,0:T(8,128)(2,1)} %finish.1), calls=%async_computation.3 | async-start | bytes 393216 | tf_op jit(solution)/shard_map/all_to_all | solution.py:345

commit v6 on v5

--- a/solution.py
+++ b/solution.py
@@ -324,17 +324,17 @@
 def finish_kernel(partner, own, back, low, out):
     total = own[...] + back[partner_entry(partner)].astype(jnp.float32)
     out[0] = total.astype(out.dtype)
-    for i in range(1, KV_HEADS):
-        out[i] = low[i]
 
 
 def finish(partner, own, back, low):
     return pl.pallas_call(
         finish_kernel,
+        grid=(1,),
         out_shape=jax.ShapeDtypeStruct(low.shape, jnp.bfloat16),
-        in_specs=[SMEM, VMEM, VMEM, VMEM],
-        out_specs=VMEM,
-        cost_estimate=pl.CostEstimate(flops=0, transcendentals=0, bytes_accessed=2**18),
+        in_specs=[SMEM, VMEM, VMEM, pl.BlockSpec(memory_space=pl.ANY)],
+        out_specs=pl.BlockSpec((1, PROMPT, KV), lambda i: (0, 0, 0)),
+        input_output_aliases={3: 0},
+        cost_estimate=pl.CostEstimate(flops=0, transcendentals=0, bytes_accessed=2**17),
         compiler_params=SMALL,
         name="finish",
     )(partner, own, back, low)

time: 139 us -> 139 us (level)
  no operation moved by 1% of the time
where the time goes in v6:
time: 139 us
  blocking collectives  82.6 us (59%)
  starting transfers between devices  25.3 us (18%)
  waiting for transfers between devices  16.1 us (12%)
  Pallas kernels  11.9 us (9%)
  local copies, waits for them, and re-layouts  1.93 us (1%)
    all_gather x2, blocking collectives, exchange(): wanted = pick(partner, lax.all_gather(block, ('z', 'core')))  57 us
    all_gather x2, blocking collectives, exchange(): return lax.all_gather(wanted, 'x', axis=0, tiled=True)  25.7 us
    all_to_all x4, starting transfers between devices, swap(): lax.all_to_all(array, 'head', split_axis=0, concat_axis=0, tiled=True)  25.3 us
    all_to_all x4, waiting for transfers between devices, swap(): lax.all_to_all(array, 'head', split_axis=0, concat_axis=0, tiled=True)  16.1 us
    pallas_call x1, Pallas kernels, attention(): pl.pallas_call(attention_kernel, out_shape=(jax.ShapeDtypeStruct(packed.s...  4.59 us
  transfers between devices with their start and end apart: 4, of which 2 were waited for; matrix products, arithmetic and copies ran while one was open for 0% of the time, Pallas kernels for 3%

profile of v6, /device:TPU:2, one launch (start us, length us, event | category | flops | bytes accessed | tf_op | source)
XLA Modules:
  0.0 138.5 jit_solution(12963411501135903652)
XLA Ops:
  0.6 0.0 copy-start
  0.6 1.7 %lay_out.1 = bf16[8,48,256]{2,1,0:T(8,128)(2,1)} custom-call(bf16[128,1024]{1,0:T(8,128)(2,1)} %keys.3, bf16[128,1024]{1,0:T(8,128)(2,1)} %values.3), custom_call_target="tpu_custom_call" | custom-call | bytes 524288 | tf_op jit(solution)/shard_map/lay_out/pallas_call | solution.py:247
  2.4 7.1 %all-to-all-start.1 = ((bf16[8,48,256]{2,1,0:T(8,128)(2,1)}), bf16[8,48,256]{2,1,0:T(8,128)(2,1)S(1)}, u32[]{:S(2)}, u32[]{:S(2)}) async-start(bf16[8,48,256]{2,1,0:T(8,128)(2,1)} %lay_out.1), calls=%async_computation.1 | async-start | bytes 393216 | tf_op jit(solution)/shard_map/all_to_all | solution.py:345
  9.5 0.0 copy-done
  9.5 0.0 copy-start.1
  9.5 0.9 copy-done.1
  10.4 0.0 copy-start.2
  10.4 0.9 copy-done.2
  11.4 1.2 pack.1
  12.6 0.0 copy-start.3
  12.6 7.3 %all-to-all-done.1.low = bf16[8,48,256]{2,1,0:T(8,128)(2,1)S(1)} async-done(((bf16[8,48,256]{2,1,0:T(8,128)(2,1)}), bf16[8,48,256]{2,1,0:T(8,128)(2,1)S(1)}, u32[]{:S(2)}, u32[]{:S(2)}) %all-to-all-start.1) | async-done | bytes 196640 | tf_op jit(solution)/shard_map/all_to_all | solution.py:345
  20.0 3.6 %all-to-all-start = ((bf16[8,336,256]{2,1,0:T(8,128)(2,1)}), bf16[8,336,256]{2,1,0:T(8,128)(2,1)S(1)}, u32[]{:S(2)}, u32[]{:S(2)}) async-start(bf16[8,336,256]{2,1,0:T(8,128)(2,1)} %pack.1), calls=%async_computation | async-start | bytes 2752512 | tf_op jit(solution)/shard_map/all_to_all | solution.py:345
  23.5 0.0 copy-start.4
  23.5 0.0 copy-start.5
  23.6 0.0 copy-start.6
  23.6 0.0 copy-start.7
  23.6 34.8 %all_gather.15.blocks = bf16[24,48,256]{2,1,0:T(8,128)(2,1)S(1)} all-gather(bf16[1,48,256]{2,1,0:T(8,128)(2,1)S(1)} %slice.4), channel_id=1, replica_groups=mesh['x'=4,'z'=12,'core'=2,'head'=8] {'z','core'}, dimensions={0}, use_global_device_ids=true | all-gather | bytes 614400 | tf_op jit(solution)/shard_map/all_gather | solution.py:229
  58.4 0.0 copy-done.3
  58.4 0.6 pick.2
  59.0 13.0 %all_gather.16.far_in = bf16[16,48,256]{2,1,0:T(8,128)(2,1)S(1)} all-gather(bf16[4,48,256]{2,1,0:T(8,128)(2,1)S(1)} %pick.2), channel_id=1, replica_groups=mesh['x'=4,'z'=12,'core'=2,'head'=8] {'x'}, dimensions={0}, use_global_device_ids=true | all-gather | bytes 491520 | tf_op jit(solution)/shard_map/all_gather | solution.py:230
  72.0 0.0 all-to-all-done.packed
  72.0 0.0 copy-done.4
  72.0 0.0 copy-done.5
  72.0 0.0 copy-done.6
  72.0 0.0 copy-done.7
  72.0 4.6 %attention.1 = (bf16[8,336,256]{2,1,0:T(8,128)(2,1)}, bf16[8,48,256]{2,1,0:T(8,128)(2,1)}, bf16[48,256]{1,0:T(8,128)(2,1)S(1)}, f32[48,256]{1,0:T(8,128)S(1)}) custom-call(s32[96]{0:T(128)S(1)} %copy-done.3, s32[1,8]{1,0:T(1,128)S(1)} %copy-done.5, s32[1,8]{1,0:T(1,128)S(1)} %copy-done.6, f32[1,8]{1,0:T(1,128)S(1)} %copy-done.7, ...), custom_call_target="tpu_custom_call" | custom-call | flops 1000000000 | bytes 5242880 | tf_op jit(solution)/shard_map/attention/pallas_call | solution.py:184
  76.6 7.1 %all-to-all-start.2 = ((bf16[8,336,256]{2,1,0:T(8,128)(2,1)}), bf16[8,336,256]{2,1,0:T(8,128)(2,1)S(1)}, u32[]{:S(2)}, u32[]{:S(2)}) async-start(bf16[8,336,256]{2,1,0:T(8,128)(2,1)} %get-tuple-element.14), calls=%async_computation.2 | async-start | bytes 2752512 | tf_op jit(solution)/shard_map/all_to_all | solution.py:345
  83.7 22.1 %all-gather = bf16[1152,256]{1,0:T(8,128)(2,1)S(1)} all-gather(bf16[48,256]{1,0:T(8,128)(2,1)S(1)} %get-tuple-element.12), channel_id=2, replica_groups=mesh['x'=4,'z'=12,'core'=2,'head'=8] {'z','core'}, dimensions={0}, use_global_device_ids=true | all-gather | bytes 614400 | tf_op jit(solution)/shard_map/all_gather | solution.py:229
  105.8 0.6 pick.3
  106.4 12.7 %all_gather.19.back = bf16[16,48,256]{2,1,0:T(8,128)(2,1)S(1)} all-gather(bf16[4,48,256]{2,1,0:T(8,128)(2,1)S(1)} %pick.3), channel_id=1, replica_groups=mesh['x'=4,'z'=12,'core'=2,'head'=8] {'x'}, dimensions={0}, use_global_device_ids=true | all-gather | bytes 491520 | tf_op jit(solution)/shard_map/all_gather | solution.py:230
  119.1 1.2 finish.1
  120.3 0.0 all-to-all-done.2.grads.rest
  120.3 7.5 %all-to-all-start.3 = ((bf16[8,48,256]{2,1,0:T(8,128)(2,1)}), bf16[8,48,256]{2,1,0:T(8,128)(2,1)S(1)}, u32[]{:S(2)}, u32[]{:S(2)}) async-start(bf16[8,48,256]{2,1,0:T(8,128)(2,1)} %finish.1), calls=%async_computation.3 | async-start | bytes 393216 | tf_op jit(solution)/shard_map/all_to_all | solution.py:345
  127.8 1.1 q_by_token.1
  128.8 8.7 %all-to-all-done.3.low = bf16[8,48,256]{2,1,0:T(8,128)(2,1)S(1)} async-done(((bf16[8,48,256]{2,1,0:T(8,128)(2,1)}), bf16[8,48,256]{2,1,0:T(8,128)(2,1)S(1)}, u32[]{:S(2)}, u32[]{:S(2)}) %all-to-all-start.3) | async-done | bytes 196640 | tf_op jit(solution)/shard_map/all_to_all | solution.py:345
  137.6 1.0 kv_by_token.1
  (1 shorter events, 0.0 us)
Async XLA Ops:
  0.6 8.9 %copy-start = (bf16[128,4096]{1,0:T(8,128)(2,1)S(1)}, bf16[128,4096]{1,0:T(8,128)(2,1)}, u32[]{:S(2)}) copy-start(bf16[128,4096]{1,0:T(8,128)(2,1)} %queries.1) | copy-start | bytes 3145732
  2.4 17.6 %all-to-all-start.1 = ((bf16[8,48,256]{2,1,0:T(8,128)(2,1)}), bf16[8,48,256]{2,1,0:T(8,128)(2,1)S(1)}, u32[]{:S(2)}, u32[]{:S(2)}) async-start(bf16[8,48,256]{2,1,0:T(8,128)(2,1)} %lay_out.1), calls=%async_computation.1 | async-start | bytes 393216 | tf_op jit(solution)/shard_map/all_to_all | solution.py:345
  9.5 1.0 copy-start.1
  10.4 0.9 copy-start.2
  12.6 45.8 %copy-start.3 = (s32[96]{0:T(128)S(1)}, s32[96]{0:T(128)}, u32[]{:S(2)}) copy-start(s32[96]{0:T(128)} %partner.7) | copy-start | bytes 1156
  20.0 52.0 %all-to-all-start = ((bf16[8,336,256]{2,1,0:T(8,128)(2,1)}), bf16[8,336,256]{2,1,0:T(8,128)(2,1)S(1)}, u32[]{:S(2)}, u32[]{:S(2)}) async-start(bf16[8,336,256]{2,1,0:T(8,128)(2,1)} %pack.1), calls=%async_computation | async-start | bytes 2752512 | tf_op jit(solution)/shard_map/all_to_all | solution.py:345
  23.5 48.5 %copy-start.4 = (bf16[1024,512]{1,0:T(8,128)(2,1)S(1)}, bf16[1024,512]{1,0:T(8,128)(2,1)}, u32[]{:S(2)}) copy-start(bf16[1024,512]{1,0:T(8,128)(2,1)} %cot_ref.1) | copy-start | bytes 3145732
  23.5 48.5 %copy-start.5 = (s32[1,8]{1,0:T(1,128)S(1)}, s32[1,8]{1,0:T(1,128)}, u32[]{:S(2)}) copy-start(s32[1,8]{1,0:T(1,128)} %lengths.1) | copy-start | bytes 100
  23.6 48.5 %copy-start.6 = (s32[1,8]{1,0:T(1,128)S(1)}, s32[1,8]{1,0:T(1,128)}, u32[]{:S(2)}) copy-start(s32[1,8]{1,0:T(1,128)} %guests.1) | copy-start | bytes 100
  23.6 48.5 %copy-start.7 = (f32[1,8]{1,0:T(1,128)S(1)}, f32[1,8]{1,0:T(1,128)}, u32[]{:S(2)}) copy-start(f32[1,8]{1,0:T(1,128)} %adv.1) | copy-start | bytes 100
  76.6 43.7 %all-to-all-start.2 = ((bf16[8,336,256]{2,1,0:T(8,128)(2,1)}), bf16[8,336,256]{2,1,0:T(8,128)(2,1)S(1)}, u32[]{:S(2)}, u32[]{:S(2)}) async-start(bf16[8,336,256]{2,1,0:T(8,128)(2,1)} %get-tuple-element.14), calls=%async_computation.2 | async-start | bytes 2752512 | tf_op jit(solution)/shard_map/all_to_all | solution.py:345
  120.3 17.3 %all-to-all-start.3 = ((bf16[8,48,256]{2,1,0:T(8,128)(2,1)}), bf16[8,48,256]{2,1,0:T(8,128)(2,1)S(1)}, u32[]{:S(2)}, u32[]{:S(2)}) async-start(bf16[8,48,256]{2,1,0:T(8,128)(2,1)} %finish.1), calls=%async_computation.3 | async-start | bytes 393216 | tf_op jit(solution)/shard_map/all_to_all | solution.py:345
